TPU v7x, 32 devices: a whole 2x2x4 slice. The times are simulated.
32 devices in a mesh: leaf: 8 (over z, x), task: 4 (over y, core).
Axes of the slice: x: 2, y: 2, z: 4, core: 2. Of those that a mesh axis runs over, the one named last changes fastest.
Arguments:
- points: bfloat16 [131072, 64], P(('leaf', 'task')), may hold values from -6 to 6
- weights: bfloat16 [131072, 64], P(('leaf', 'task')), may hold values from -4 to 4
- point_order: int32 [8, 4, 4096], P('leaf', 'task'), may hold values from 0 to 4095, each once within a row
- node_order: int32 [8, 4, 4096], P('leaf', 'task'), may hold values from 0 to 4095, each once within a row
- merge_order: int32 [8, 4, 2, 1024], P('leaf', 'task'), may hold values from 0 to 1023, as said below
- far_list: int32 [8, 4, 4, 3], P('leaf', 'task'), may hold values 0 or 1
- task_target: int32 [8, 4, 4, 1], P('leaf', 'task'), may hold values from -1 to 3, as said below
- task_source: int32 [8, 4, 4, 1], P('leaf', 'task'), may hold values from 0 to 3
Outputs:
- potentials: float32 [131072, 64], P(('leaf', 'task'))
Inputs may be any that keep to these rules, and one draw needn't show every extreme that they name: `merge_order`: each row is a permutation of 0 to 1023; rows [i, j, b] are equal for all i with the same i // 2 ** (b + 1). `task_target`: -1 marks an empty slot; every device of every draw has a slab toward which all 1 slots are used.
All inputs are finite; a program needn't handle non-finite values. No bound on the sum of `far_list` on one device may be relied on, other than what follows from the above.
Results may differ from a plain program's by a relative error of at most 0.002.
Values may be sent and summed in bfloat16 or wider, within the bound.
A program may use at most 64 MiB of HBM per device.

v0:
```python
import jax
import jax.numpy as jnp
from jax import lax
from jax.sharding import PartitionSpec as P

LEAF_PTS = 1024
SKEL = 512
LEVELS = 3
LEAF_DEV = 4


KERNEL_SCALE = 1.5


def partner(value, axis, stride):
    mask = 2**stride
    pairs = [(source, source ^ mask) for source in range(lax.axis_size(axis))]
    return lax.ppermute(value, axis, pairs)


def kernel(left_pts, right_pts):
    cross_term = jnp.einsum(
        "...mf,...nf->...mn", left_pts, right_pts, preferred_element_type=jnp.float32
    )
    left_norm = jnp.sum(jnp.square(left_pts.astype(jnp.float32)), axis=-1)
    right_norm = jnp.sum(jnp.square(right_pts.astype(jnp.float32)), axis=-1)
    distance = left_norm[..., :, None] + right_norm[..., None, :] - 2.0 * cross_term
    return jnp.exp(-KERNEL_SCALE / left_pts.shape[-1] * distance)


def anterpolate(skel_x, rest_x, skel_w, rest_w):
    dense = kernel(skel_x, rest_x)
    spread = (dense / jnp.sum(dense, axis=0, keepdims=True)).astype(jnp.bfloat16)
    summed = skel_w.astype(jnp.float32) + jnp.dot(
        spread, rest_w, preferred_element_type=jnp.float32
    )
    return summed.astype(jnp.bfloat16)


def merge_joined(picked, features):
    head = picked[:SKEL]
    tail = picked[SKEL:]
    merged_w = anterpolate(
        head[:, :features], tail[:, :features], head[:, features:], tail[:, features:]
    )
    return jnp.concatenate([head[:, :features], merged_w], axis=1)


def pair_terms(target_x, source_x, source_w):
    dense = kernel(target_x, source_x).astype(jnp.bfloat16)
    return jnp.einsum("ktu,kue->kte", dense, source_w, preferred_element_type=jnp.float32)


def body(points, weights, point_order, node_order, merge_order, far_list, task_target, task_source):
    features = points.shape[1]
    columns = weights.shape[1]
    point_rows = points.shape[0]
    joined = jnp.concatenate([points, weights], axis=1)
    width = joined.shape[1]
    tree = joined[point_order[0, 0]]
    node = merge_joined(tree[node_order[0, 0]], features)
    position = lax.axis_index("leaf")
    siblings = []
    for level_index in range(LEVELS):
        other = partner(node, "leaf", level_index)
        siblings.append(other)
        if level_index < LEVELS - 1:
            upper = position >> level_index & 1 == 1
            cat_rows = jnp.where(
                upper,
                jnp.concatenate([other, node], axis=0),
                jnp.concatenate([node, other], axis=0),
            )
            node = merge_joined(cat_rows[merge_order[0, 0, level_index]], features)
    tree_x = tree[:, :features]
    far_field = jnp.zeros((LEAF_DEV, LEAF_PTS, columns), jnp.float32)
    for level_index in range(LEVELS):
        other = siblings[level_index]
        dense = kernel(tree_x, other[:, :features]).astype(jnp.bfloat16)
        far_part = jnp.dot(dense, other[:, features:], preferred_element_type=jnp.float32)
        flags = far_list[0, 0, :, level_index].astype(jnp.float32)
        far_field = far_field + far_part.reshape(LEAF_DEV, LEAF_PTS, columns) * flags[:, None, None]
    leaves = tree.reshape(LEAF_DEV, LEAF_PTS, width)
    target = task_target[0, 0]
    source = task_source[0, 0]
    is_live = target >= 0
    slot_leaf = jnp.maximum(target, 0)
    requested = lax.all_to_all(source, "task", split_axis=0, concat_axis=0, tiled=True)
    arrived = lax.all_to_all(leaves[requested], "task", split_axis=0, concat_axis=0, tiled=True)

    def local_peer(group):
        own_rows, peer_rows = group
        return pair_terms(
            own_rows[..., :features], peer_rows[..., :features], peer_rows[..., features:]
        )

    slot_terms = lax.map(local_peer, (leaves[slot_leaf], arrived))
    onehot = (
        (slot_leaf[..., None] == jnp.arange(LEAF_DEV)[None, None, :]) & is_live[..., None]
    ).astype(jnp.float32)
    near_field = jnp.einsum("pcl,pcte->lte", onehot, slot_terms, precision=lax.Precision.HIGHEST)
    return (far_field + near_field).reshape(point_rows, columns)


def solution(mesh):
    return jax.shard_map(
        body,
        mesh=mesh,
        in_specs=(
            P(("leaf", "task"), None),
            P(("leaf", "task"), None),
            P("leaf", "task", None),
            P("leaf", "task", None),
            P("leaf", "task", None, None),
            P("leaf", "task", None, None),
            P("leaf", "task", None, None),
            P("leaf", "task", None, None),
        ),
        out_specs=P(("leaf", "task"), None),
        check_vma=False,
    )
```

profile of v0, /device:TPU:0, one launch (start us, length us, event | category | flops | bytes accessed | tf_op | source)
XLA Modules:
  0.0 122.4 jit_solution(18429815038106257094)
XLA Ops:
  0.0 1.5 %copy.46 = bf16[4096,64]{1,0:T(8,128)(2,1)S(1)} copy(bf16[4096,64]{0,1:T(8,128)(2,1)} %param.10) | data formatting | bytes 1048576 | tf_op args[0]
  1.5 1.5 %copy.47 = bf16[4096,64]{1,0:T(8,128)(2,1)S(1)} copy(bf16[4096,64]{0,1:T(8,128)(2,1)} %param.11) | data formatting | bytes 1048576 | tf_op args[1]
  3.0 0.7 compare_select_fusion.1
  3.8 0.7 compare_select_fusion
  4.6 0.6 pad_maximum_fusion
  5.1 12.1 %gather_fusion = bf16[4096,128]{1,0:T(8,128)(2,1)S(1)} fusion(bf16[4096,128]{1,0:T(8,128)(2,1)S(1)} %pad_maximum_fusion, s32[4096]{0:T(1024)S(1)} %broadcast_clamp_fusion.1), kind=kCustom, calls=%fused_computation | custom fusion | bytes 2113536 | tf_op jit(solution)/shard_map/gather | solution.py:60
  17.3 12.1 %gather_fusion.1 = bf16[4096,128]{1,0:T(8,128)(2,1)S(1)} fusion(bf16[4096,128]{1,0:T(8,128)(2,1)S(1)} %gather_fusion, s32[4096]{0:T(1024)S(1)} %broadcast_clamp_fusion), kind=kCustom, calls=%fused_computation.1 | custom fusion | bytes 2113536 | tf_op jit(solution)/shard_map/gather | solution.py:61
  29.5 0.5 multiply_reduce_fusion.3
  30.3 2.0 %fusion.68 = (f32[3584]{0:T(1024)S(1)}, f32[512,3584]{1,0:T(8,128)S(1)}) fusion(bf16[4096,128]{1,0:T(8,128)(2,1)S(1)} %gather_fusion.1, f32[3584]{0:T(1024)S(1)} %multiply_reduce_fusion.3, f32[512]{0:T(512)S(1)} %multiply_reduce_fusion.11), kind=kOutput, calls=%fused_computation.114 | convolution fusion | flops 244052480 | bytes 8419328 | tf_op jit(solution)/shard_map/...mf,...nf->...mn/dot_general | solution.py:22
  32.4 1.6 %fusion.24 = bf16[512,64]{0,1:T(8,128)(2,1)S(1)} fusion(f32[512,3584]{1,0:T(8,128)S(1)} %get-tuple-element.50, f32[3584]{0:T(1024)S(1)} %get-tuple-element.49, bf16[4096,128]{1,0:T(8,128)(2,1)S(1)} %gather_fusion.1, bf16[512,64]{0,1:T(8,128)(2,1)S(1)} %copy.62), kind=kOutput, calls=%fused_computation.43 | convolution fusion | flops 238649344 | bytes 8404992 | tf_op jit(solution)/shard_map/dot_general | solution.py:34
  34.0 3.0 %collective-permute-start = (bf16[512,128]{0,1:T(8,128)(2,1)S(1)}, bf16[512,128]{0,1:T(8,128)(2,1)S(1)}, u32[]{:S(2)}, u32[]{:S(2)}) collective-permute-start(bf16[512,128]{0,1:T(8,128)(2,1)S(1)} %pad_maximum_fusion.1), channel_id=1, source_target_pairs={{0,4},{4,0},{8,12},{12,8},{16,20},{20,16},{24,28},{28,24},{1,5},{5... | collective-permute-start | bytes 393224 | tf_op jit(solution)/shard_map/ppermute | solution.py:18
  37.0 0.7 copy.56
  37.7 3.2 %all-to-all-start = ((s32[4,1,1]{2,1,0:T(1,128)}), s32[4,1,1]{2,1,0:T(1,128)S(1)}, u32[]{:S(2)}, u32[]{:S(2)}) async-start(s32[4,1,1]{2,1,0:T(1,128)} %copy.56), calls=%async_computation | async-start | bytes 4096 | tf_op jit(solution)/shard_map/all_to_all | solution.py:88
  40.9 0.6 multiply_reduce_fusion.2
  41.6 0.6 compare_bitcast_fusion
  42.2 0.6 broadcast_clamp_fusion.3
  42.8 0.6 broadcast_clamp_fusion.2
  43.4 0.6 convert_bitcast_fusion.2
  44.0 0.7 gather_fusion.4
  44.7 0.2 fusion.50
  44.9 1.7 %gather_fusion.5 = bf16[4,1024,128]{2,1,0:T(8,128)(2,1)} fusion(bf16[4,1024,128]{2,1,0:T(8,128)(2,1)S(1)} %bitcast.72, s32[1024]{0:T(1024)S(1)} %pad_clamp_fusion), kind=kCustom, calls=%fused_computation.5 | custom fusion | bytes 2097168 | tf_op jit(solution)/shard_map/gather | solution.py:89
  46.6 3.7 %all-to-all-start.1 = ((bf16[4,1,1024,128]{3,2,1,0:T(8,128)(2,1)}), bf16[4,1,1024,128]{3,2,1,0:T(8,128)(2,1)S(1)}, u32[]{:S(2)}, u32[]{:S(2)}) async-start(bf16[4,1,1024,128]{3,2,1,0:T(8,128)(2,1)} %bitcast.74), calls=%async_computation.1 | async-start | bytes 2097152 | tf_op jit(solution)/shard_map/all_to_all | solution.py:89
  50.4 0.6 copy-done
  51.0 0.8 maximum_select_fusion
  51.8 1.1 copy.50
  52.9 4.6 %gather_fusion.2 = bf16[1024,128]{1,0:T(8,128)(2,1)} fusion(bf16[1024,128]{1,0:T(8,128)(2,1)S(1)} %copy.50, s32[1024]{0:T(1024)} %broadcast_clamp_fusion.3), kind=kCustom, calls=%fused_computation.2 | custom fusion | bytes 528384 | tf_op jit(solution)/shard_map/gather | solution.py:74
  57.5 1.1 fusion.67
  58.6 1.1 multiply_reduce_fusion.5
  59.9 1.4 %fusion.69 = (f32[512]{0:T(512)S(1)}, f32[512,512]{1,0:T(8,128)S(1)}) fusion(bf16[1024,128]{1,0:T(8,128)(2,1)} %gather_fusion.2, f32[512]{0:T(512)S(1)} %multiply_reduce_fusion.5, f32[512]{0:T(512)S(1)} %multiply_reduce_fusion.9), kind=kOutput, calls=%fused_computation.115 | convolution fusion | flops 34864640 | bytes 1316864 | tf_op jit(solution)/shard_map/...mf,...nf->...mn/dot_general | solution.py:22
  61.3 1.3 %fusion.25 = bf16[512,64]{0,1:T(8,128)(2,1)S(1)} fusion(f32[512,512]{1,0:T(8,128)S(1)} %get-tuple-element.52, f32[512]{0:T(512)S(1)} %get-tuple-element.51, bf16[1024,128]{1,0:T(8,128)(2,1)} %gather_fusion.2, bf16[512,64]{0,1:T(8,128)(2,1)S(1)} %copy.64), kind=kOutput, calls=%fused_computation.44 | convolution fusion | flops 34177024 | bytes 1312768 | tf_op jit(solution)/shard_map/dot_general | solution.py:34
  62.6 1.6 %collective-permute-start.1 = (bf16[512,128]{0,1:T(8,128)(2,1)S(1)}, bf16[512,128]{0,1:T(8,128)(2,1)S(1)}, u32[]{:S(2)}, u32[]{:S(2)}) collective-permute-start(bf16[512,128]{0,1:T(8,128)(2,1)S(1)} %pad_maximum_fusion.2), channel_id=1, source_target_pairs={{0,8},{4,12},{8,0},{12,4},{16,24},{20,28},{24,16},{28,20},{1,9},{5... | collective-permute-start | bytes 393224 | tf_op jit(solution)/shard_map/ppermute | solution.py:18
  64.2 1.5 %multiply_reduce_fusion.10 = f32[512]{0:T(512)} fusion(bf16[512,128]{0,1:T(8,128)(2,1)} %copy-done), kind=kLoop, calls=%fused_computation.70 | loop fusion | flops 97792 | bytes 67584 | tf_op jit(solution)/shard_map/reduce_sum | solution.py:26
  65.7 4.7 %fusion.14 = f32[4096,64]{0,1:T(8,128)} fusion(f32[512]{0:T(512)} %multiply_reduce_fusion.10, f32[4096]{0:T(1024)S(1)} %multiply_reduce_fusion.2, bf16[4096,128]{1,0:T(8,128)(2,1)S(1)} %gather_fusion, bf16[512,128]{0,1:T(8,128)(2,1)} %copy-done), kind=kOutput, calls=%fused_computation.29 | convolution fusion | flops 547356672 | bytes 2246656 | tf_op jit(solution)/shard_map/dot_general | solution.py:80
  70.4 2.9 %reshape.299 = f32[4,1024,64]{1,0,2:T(4,128)} reshape(f32[4096,64]{0,1:T(8,128)} %fusion.14) | data formatting | bytes 2097152 | tf_op jit(solution)/shard_map/reshape | solution.py:82
  73.4 0.6 copy-done.1
  74.0 0.8 maximum_select_fusion.1
  74.8 1.1 copy.53
  75.9 4.6 %gather_fusion.3 = bf16[1024,128]{1,0:T(8,128)(2,1)} fusion(bf16[1024,128]{1,0:T(8,128)(2,1)S(1)} %copy.53, s32[1024]{0:T(1024)} %broadcast_clamp_fusion.2), kind=kCustom, calls=%fused_computation.3 | custom fusion | bytes 528384 | tf_op jit(solution)/shard_map/gather | solution.py:74
  80.6 1.1 fusion.66
  81.7 1.1 multiply_reduce_fusion.4
  82.9 1.4 %fusion.70 = (f32[512]{0:T(512)S(1)}, f32[512,512]{1,0:T(8,128)S(1)}) fusion(bf16[1024,128]{1,0:T(8,128)(2,1)} %gather_fusion.3, f32[512]{0:T(512)S(1)} %multiply_reduce_fusion.4, f32[512]{0:T(512)S(1)} %multiply_reduce_fusion.7), kind=kOutput, calls=%fused_computation.116 | convolution fusion | flops 34864640 | bytes 1316864 | tf_op jit(solution)/shard_map/...mf,...nf->...mn/dot_general | solution.py:22
  84.3 1.3 %fusion.26 = bf16[512,64]{0,1:T(8,128)(2,1)S(1)} fusion(f32[512,512]{1,0:T(8,128)S(1)} %get-tuple-element.54, f32[512]{0:T(512)S(1)} %get-tuple-element.53, bf16[1024,128]{1,0:T(8,128)(2,1)} %gather_fusion.3, bf16[512,64]{0,1:T(8,128)(2,1)S(1)} %copy.66), kind=kOutput, calls=%fused_computation.45 | convolution fusion | flops 34177024 | bytes 1312768 | tf_op jit(solution)/shard_map/dot_general | solution.py:34
  85.6 2.7 %collective-permute-start.2 = (bf16[512,128]{0,1:T(8,128)(2,1)S(1)}, bf16[512,128]{0,1:T(8,128)(2,1)S(1)}, u32[]{:S(2)}, u32[]{:S(2)}) collective-permute-start(bf16[512,128]{0,1:T(8,128)(2,1)S(1)} %pad_maximum_fusion.3), channel_id=1, source_target_pairs={{0,16},{4,20},{8,24},{12,28},{16,0},{20,4},{24,8},{28,12},{1,17},{... | collective-permute-start | bytes 393224 | tf_op jit(solution)/shard_map/ppermute | solution.py:18
  88.3 0.9 multiply_reduce_fusion.8
  89.2 4.7 %fusion.15 = f32[4096,64]{0,1:T(8,128)} fusion(f32[512]{0:T(512)S(1)} %multiply_reduce_fusion.8, f32[4096]{0:T(1024)S(1)} %multiply_reduce_fusion.2, bf16[4096,128]{1,0:T(8,128)(2,1)S(1)} %gather_fusion, bf16[512,128]{0,1:T(8,128)(2,1)} %copy-done.1), kind=kOutput, calls=%fused_computation.30 | convolution fusion | flops 547356672 | bytes 2246656 | tf_op jit(solution)/shard_map/dot_general | solution.py:80
  93.9 2.9 %reshape.300 = f32[4,1024,64]{1,0,2:T(4,128)} reshape(f32[4096,64]{0,1:T(8,128)} %fusion.15) | data formatting | bytes 2097152 | tf_op jit(solution)/shard_map/reshape | solution.py:82
  96.8 3.8 %fusion.16 = f32[4096,64]{0,1:T(8,128)} fusion(f32[512]{0:T(512)S(1)} %multiply_reduce_fusion.6, f32[4096]{0:T(1024)S(1)} %multiply_reduce_fusion.2, bf16[4096,128]{1,0:T(8,128)(2,1)S(1)} %gather_fusion, bf16[512,128]{0,1:T(8,128)(2,1)S(1)} %collective-permute-done.2), kind=kOutput, calls=%fused_computation.31 | convolution fusion | flops 547356672 | bytes 2246656 | tf_op jit(solution)/shard_map/dot_general | solution.py:80
  100.7 2.9 %reshape.301 = f32[4,1024,64]{1,0,2:T(4,128)} reshape(f32[4096,64]{0,1:T(8,128)} %fusion.16) | data formatting | bytes 2097152 | tf_op jit(solution)/shard_map/reshape | solution.py:82
  103.6 11.1 %while.10 = (s32[]{:T(128)}, f32[4,1,1024,64]{2,3,1,0:T(8,128)}, bf16[4,1,1024,128]{3,2,1,0:T(8,128)(2,1)S(1)}, bf16[4,1,1024,128]{3,2,1,0:T(8,128)(2,1)S(1)}, s32[]{:T(128)}) while((s32[]{:T(128)}, f32[4,1,1024,64]{2,3,1,0:T(8,128)}, bf16[4,1,1024,128]{3,2,1,0:T(8,128)(2,1)S(1)}, bf16[4,1,1024,128]{3,2,1,0:T(8,128)(2,1)S(1)}, ...), condition=%wide.region_16.17_spmd, body=%wide.region_13.16_spmd.sunk | while | flops 274069504 | bytes 2376257 | solution.py:97
  103.7 0.2 multiply_reduce_fusion.14
  103.9 0.2 multiply_reduce_fusion.15
  104.1 2.3 %fusion.76 = f32[4,1,1024,64]{2,3,1,0:T(8,128)} fusion(f32[4,1,1024,64]{2,3,1,0:T(8,128)} %get-tuple-element.90, s32[]{:T(128)} %get-tuple-element.89, f32[1024]{0:T(1024)S(1)} %multiply_reduce_fusion.14, f32[1024]{0:T(1024)S(1)} %multiply_reduce_fusion.15, bf16[1,1024,128]{2,1,0:T(8,128)(2,1)S(1)} %get-tuple-element.82, ...), kind=kOutput, calls=%fused_computation.9.clone.1 | convolution fusion | flops 273678336 | bytes 1057280 | tf_op jit(solution)/shard_map/while/body/eval_jaxpr/ktu,kue->kte/dot_general | solution.py:51
  106.5 0.2 multiply_reduce_fusion.14
  106.7 0.2 multiply_reduce_fusion.15
  106.9 2.3 %fusion.76 = f32[4,1,1024,64]{2,3,1,0:T(8,128)} fusion(f32[4,1,1024,64]{2,3,1,0:T(8,128)} %get-tuple-element.90, s32[]{:T(128)} %get-tuple-element.89, f32[1024]{0:T(1024)S(1)} %multiply_reduce_fusion.14, f32[1024]{0:T(1024)S(1)} %multiply_reduce_fusion.15, bf16[1,1024,128]{2,1,0:T(8,128)(2,1)S(1)} %get-tuple-element.82, ...), kind=kOutput, calls=%fused_computation.9.clone.1 | convolution fusion | flops 273678336 | bytes 1057280 | tf_op jit(solution)/shard_map/while/body/eval_jaxpr/ktu,kue->kte/dot_general | solution.py:51
  109.2 0.2 multiply_reduce_fusion.14
  109.4 0.2 multiply_reduce_fusion.15
  109.7 2.3 %fusion.76 = f32[4,1,1024,64]{2,3,1,0:T(8,128)} fusion(f32[4,1,1024,64]{2,3,1,0:T(8,128)} %get-tuple-element.90, s32[]{:T(128)} %get-tuple-element.89, f32[1024]{0:T(1024)S(1)} %multiply_reduce_fusion.14, f32[1024]{0:T(1024)S(1)} %multiply_reduce_fusion.15, bf16[1,1024,128]{2,1,0:T(8,128)(2,1)S(1)} %get-tuple-element.82, ...), kind=kOutput, calls=%fused_computation.9.clone.1 | convolution fusion | flops 273678336 | bytes 1057280 | tf_op jit(solution)/shard_map/while/body/eval_jaxpr/ktu,kue->kte/dot_general | solution.py:51
  112.0 0.2 multiply_reduce_fusion.14
  112.2 0.2 multiply_reduce_fusion.15
  112.4 2.3 %fusion.76 = f32[4,1,1024,64]{2,3,1,0:T(8,128)} fusion(f32[4,1,1024,64]{2,3,1,0:T(8,128)} %get-tuple-element.90, s32[]{:T(128)} %get-tuple-element.89, f32[1024]{0:T(1024)S(1)} %multiply_reduce_fusion.14, f32[1024]{0:T(1024)S(1)} %multiply_reduce_fusion.15, bf16[1,1024,128]{2,1,0:T(8,128)(2,1)S(1)} %get-tuple-element.82, ...), kind=kOutput, calls=%fused_computation.9.clone.1 | convolution fusion | flops 273678336 | bytes 1057280 | tf_op jit(solution)/shard_map/while/body/eval_jaxpr/ktu,kue->kte/dot_general | solution.py:51
  114.7 3.1 %fusion.27 = f32[4,1024,64]{1,0,2:T(4,128)S(1)} fusion(f32[4,1024,64]{1,2,0:T(8,128)} %bitcast.76, s32[4]{0:T(128)S(1)} %copy-done.7, pred[4]{0:T(512)(128)(4,1)S(1)} %copy-done.10), kind=kOutput, calls=%fused_computation.47 | convolution fusion | flops 12582944 | bytes 2097172 | tf_op jit(solution)/shard_map/pcl,pcte->lte/dot_general | solution.py:101
  117.9 2.9 %add_add_fusion = f32[4,1024,64]{1,0,2:T(4,128)S(1)} fusion(f32[4,1024,64]{1,0,2:T(4,128)S(1)} %fusion.27, f32[4,1024,64]{1,0,2:T(4,128)} %reshape.301, f32[4,1024,64]{1,0,2:T(4,128)} %reshape.300, f32[4,1024,64]{1,0,2:T(4,128)} %reshape.299, f32[4]{0:T(128)S(1)} %copy-done.4, f32[4]{0:T(128)S(1)} %copy-done.5, f32[4]{0:T(128)S(1)} %copy-done.3), kind=kLoop, calls=%fused_computation.49 | loop fusion | flops 1572864 | bytes 5242928 | tf_op jit(solution)/shard_map/add | solution.py:102
  120.8 1.6 %copy.67 = f32[8,8,4,1024]{3,1,2,0:T(8,128)} copy(f32[8,8,4,1024]{3,2,1,0:T(4,128)S(1)} %bitcast.75) | data formatting | bytes 2097152
  (52 shorter events, 1.1 us)
Async XLA Ops:
  32.3 4.7 %copy-start.9 = (s32[1,1,4,1]{2,3,1,0:T(1,128)S(1)}, s32[1,1,4,1]{2,3,1,0:T(1,128)}, u32[]{:S(2)}) copy-start(s32[1,1,4,1]{2,3,1,0:T(1,128)} %param.17) | copy-start | bytes 52
  32.3 9.2 %copy-start.11 = (s32[1,1,4,1]{2,3,1,0:T(1,128)S(1)}, s32[1,1,4,1]{2,3,1,0:T(1,128)}, u32[]{:S(2)}) copy-start(s32[1,1,4,1]{2,3,1,0:T(1,128)} %param.16) | copy-start | bytes 52
  32.4 9.8 %copy-start.2 = (s32[1,1,2,1024]{3,2,1,0:T(2,128)S(1)}, s32[1,1,2,1024]{3,2,1,0:T(2,128)}, u32[]{:S(2)}) copy-start(s32[1,1,2,1024]{3,2,1,0:T(2,128)} %param.14) | copy-start | bytes 24580
  32.4 11.0 %copy-start.8 = (s32[1,1,4,3]{2,1,3,0:T(1,128)S(1)}, s32[1,1,4,3]{2,1,3,0:T(1,128)}, u32[]{:S(2)}) copy-start(s32[1,1,4,3]{2,1,3,0:T(1,128)} %param.15) | copy-start | bytes 148
  34.0 16.4 %collective-permute-start = (bf16[512,128]{0,1:T(8,128)(2,1)S(1)}, bf16[512,128]{0,1:T(8,128)(2,1)S(1)}, u32[]{:S(2)}, u32[]{:S(2)}) collective-permute-start(bf16[512,128]{0,1:T(8,128)(2,1)S(1)} %pad_maximum_fusion.1), channel_id=1, source_target_pairs={{0,4},{4,0},{8,12},{12,8},{16,20},{20,16},{24,28},{28,24},{1,5},{5... | collective-permute-start | bytes 393224 | tf_op jit(solution)/shard_map/ppermute | solution.py:18
  37.7 7.1 %all-to-all-start = ((s32[4,1,1]{2,1,0:T(1,128)}), s32[4,1,1]{2,1,0:T(1,128)S(1)}, u32[]{:S(2)}, u32[]{:S(2)}) async-start(s32[4,1,1]{2,1,0:T(1,128)} %copy.56), calls=%async_computation | async-start | bytes 4096 | tf_op jit(solution)/shard_map/all_to_all | solution.py:88
  41.6 5.1 %copy-start.6 = (s32[4]{0:T(128)}, s32[4]{0:T(128)S(1)}, u32[]{:S(2)}) copy-start(s32[4]{0:T(128)S(1)} %maximum_bitcast_fusion) | copy-start | bytes 52
  46.6 57.0 %all-to-all-start.1 = ((bf16[4,1,1024,128]{3,2,1,0:T(8,128)(2,1)}), bf16[4,1,1024,128]{3,2,1,0:T(8,128)(2,1)S(1)}, u32[]{:S(2)}, u32[]{:S(2)}) async-start(bf16[4,1,1024,128]{3,2,1,0:T(8,128)(2,1)} %bitcast.74), calls=%async_computation.1 | async-start | bytes 2097152 | tf_op jit(solution)/shard_map/all_to_all | solution.py:89
  50.4 0.7 copy-start
  62.6 10.8 %collective-permute-start.1 = (bf16[512,128]{0,1:T(8,128)(2,1)S(1)}, bf16[512,128]{0,1:T(8,128)(2,1)S(1)}, u32[]{:S(2)}, u32[]{:S(2)}) collective-permute-start(bf16[512,128]{0,1:T(8,128)(2,1)S(1)} %pad_maximum_fusion.2), channel_id=1, source_target_pairs={{0,8},{4,12},{8,0},{12,4},{16,24},{20,28},{24,16},{28,20},{1,9},{5... | collective-permute-start | bytes 393224 | tf_op jit(solution)/shard_map/ppermute | solution.py:18
  73.4 0.6 copy-start.1
  85.6 11.2 %collective-permute-start.2 = (bf16[512,128]{0,1:T(8,128)(2,1)S(1)}, bf16[512,128]{0,1:T(8,128)(2,1)S(1)}, u32[]{:S(2)}, u32[]{:S(2)}) collective-permute-start(bf16[512,128]{0,1:T(8,128)(2,1)S(1)} %pad_maximum_fusion.3), channel_id=1, source_target_pairs={{0,16},{4,20},{8,24},{12,28},{16,0},{20,4},{24,8},{28,12},{1,17},{... | collective-permute-start | bytes 393224 | tf_op jit(solution)/shard_map/ppermute | solution.py:18
  103.6 11.1 %copy-start.7 = (s32[4]{0:T(128)S(1)}, s32[4]{0:T(128)}, u32[]{:S(2)}) copy-start(s32[4]{0:T(128)} %copy-done.6) | copy-start | bytes 52
  103.6 11.1 %copy-start.10 = (pred[4]{0:T(512)(128)(4,1)S(1)}, pred[4]{0:T(512)(128)(4,1)}, u32[]{:S(2)}) copy-start(pred[4]{0:T(512)(128)(4,1)} %compare_bitcast_fusion) | copy-start | bytes 16
  103.6 14.3 %copy-start.3 = (f32[4]{0:T(128)S(1)}, f32[4]{0:T(128)}, u32[]{:S(2)}) copy-start(f32[4]{0:T(128)} %get-tuple-element.46) | copy-start | bytes 52
  103.6 14.3 %copy-start.4 = (f32[4]{0:T(128)S(1)}, f32[4]{0:T(128)}, u32[]{:S(2)}) copy-start(f32[4]{0:T(128)} %get-tuple-element.47) | copy-start | bytes 52
  103.6 14.3 %copy-start.5 = (f32[4]{0:T(128)S(1)}, f32[4]{0:T(128)}, u32[]{:S(2)}) copy-start(f32[4]{0:T(128)} %get-tuple-element.48) | copy-start | bytes 52
where the time goes:
time: 123 us; the launch traced here: 122 us
  local copies, waits for them, and re-layouts  56.6 us (46%)
  matrix products  34.5 us (28%)
  other arithmetic  16.5 us (13%)
  starting transfers between devices  14.3 us (12%)
    dot_general x3, matrix products, body(): jnp.dot(dense, other[:, features:], preferred_element_type=jnp.float32)  13.3 us
    gather x1, local copies, waits for them, and re-layouts, body(): node = merge_joined(tree[node_order[0, 0]], features)  12.1 us
    gather x1, local copies, waits for them, and re-layouts, body(): tree = joined[point_order[0, 0]]  12.1 us
    gather x2, local copies, waits for them, and re-layouts, body(): node = merge_joined(cat_rows[merge_order[0, 0, level_index]], features)  9.25 us
    dot_general x4, matrix products, pair_terms(): jnp.einsum('ktu,kue->kte', dense, source_w, preferred_element_type=jnp.fl...  9.18 us
    reshape x3, local copies, waits for them, and re-layouts, body(): far_part.reshape(LEAF_DEV, LEAF_PTS, columns) * flags[:, None, None]  8.75 us
    ppermute x3, starting transfers between devices, partner(): return lax.ppermute(value, axis, pairs)  7.33 us
    unnamed x33, local copies, waits for them, and re-layouts  6.54 us
  transfers between devices with their start and end apart: 5, of which 0 were waited for; matrix products, arithmetic and copies ran while one was open for 44% of the time, Pallas kernels for 0%

commit v1 on v0

v1 whole, which is shorter than its diff:
```python
import functools
import math

import jax
import jax.numpy as jnp
from jax import lax
from jax.experimental import pallas as pl
from jax.experimental.pallas import tpu as pltpu
from jax.sharding import PartitionSpec as P

SKEL = 512
KERNEL_SCALE = 1.5
BF = jnp.bfloat16
F32 = jnp.float32

VMEM = pl.BlockSpec(memory_space=pltpu.VMEM)
SMEM = pl.BlockSpec(memory_space=pltpu.SMEM)


def partner(value, axis, stride):
    mask = 2**stride
    pairs = [(source, source ^ mask) for source in range(lax.axis_size(axis))]
    return lax.ppermute(value, axis, pairs)


def pieces(norm):
    first = norm.astype(BF).astype(F32)
    left = norm - first
    second = left.astype(BF).astype(F32)
    third = left - second
    return first, second, third


def row_norms(rows, features):
    width = rows.shape[1]
    square = rows * rows
    high = square.astype(BF)
    low = (square - high.astype(F32)).astype(BF)
    picks = (lax.broadcasted_iota(jnp.int32, (width, width), 0) < features).astype(F32).astype(BF)
    return jnp.dot(high, picks, preferred_element_type=F32) + jnp.dot(
        low, picks, preferred_element_type=F32
    )


def placed(lanes, features, body, parts, ones_first):
    first, second, third = parts
    a, b = (3, 0) if ones_first else (0, 3)
    out = jnp.where(lanes < features, body, 0.0)
    out = jnp.where(lanes == features + a, -first, out)
    out = jnp.where(lanes == features + a + 1, -second, out)
    out = jnp.where(lanes == features + a + 2, -third, out)
    ones = (lanes >= features + b) & (lanes < features + b + 3)
    return jnp.where(ones, 1.0, out).astype(BF)


def left_rows(rows, features):
    lanes = lax.broadcasted_iota(jnp.int32, rows.shape, 1)
    return placed(lanes, features, 2.0 * rows, pieces(row_norms(rows, features)), False)


def right_rows(rows, features):
    lanes = lax.broadcasted_iota(jnp.int32, rows.shape, 1)
    return placed(lanes, features, rows, pieces(row_norms(rows, features)), True)


NT = (((1,), (1,)), ((), ()))


def dense_of(exponent, features):
    return jnp.exp2(exponent * (KERNEL_SCALE / features * math.log2(math.e)))


def spread_of(exponent, features):
    dense = dense_of(exponent, features)
    return (dense * (1.0 / jnp.sum(dense, axis=0, keepdims=True))).astype(BF)


def turned(points_ref, weights_ref, rows_ref, extra_ref=None):
    step = 512
    for start in range(0, rows_ref.shape[0], step):
        both = jnp.concatenate(
            [points_ref[:, start : start + step], weights_ref[:, start : start + step]], axis=0
        )
        block = both.astype(F32).T
        rows_ref[start : start + step, :] = block
        if extra_ref is not None:
            extra_ref[start : start + step, :] = block


def level_zero_kernel(features, points_ref, weights_ref, order_ref, node_ref, out_ref,
                      rows_ref, rest_ref, skel_ref):
    count = points_ref.shape[1]
    turned(points_ref, weights_ref, rows_ref, rest_ref)
    blank = jnp.zeros((1, rows_ref.shape[1]), F32)
    group = 16

    def pick(step, carry):
        for inner in range(group):
            at = step * group + inner
            index = order_ref[node_ref[at]]
            skel_ref[pl.ds(at, 1), :] = rows_ref[pl.ds(index, 1), :]
            rest_ref[pl.ds(index, 1), :] = blank
        return carry

    lax.fori_loop(0, SKEL // group, pick, 0)
    skel = skel_ref[...]
    left = left_rows(skel, features)
    width = rows_ref.shape[1]
    chunk = 512
    total = jnp.zeros((SKEL, width), F32)
    for start in range(0, count, chunk):
        part = points_ref[:, start : start + chunk].astype(F32)
        norm = jnp.sum(part * part, axis=0, keepdims=True)
        first, second, third = pieces(norm)
        lines = lax.broadcasted_iota(jnp.int32, (width - features, chunk), 0)
        tail = jnp.where(lines < 3, 1.0, 0.0)
        tail = jnp.where(lines == 3, -first, tail)
        tail = jnp.where(lines == 4, -second, tail)
        tail = jnp.where(lines == 5, -third, tail)
        right = jnp.concatenate([part, tail], axis=0).astype(BF)
        spread = spread_of(jnp.dot(left, right, preferred_element_type=F32), features)
        total = total + jnp.dot(
            spread, rest_ref[start : start + chunk, :].astype(BF), preferred_element_type=F32
        )
    lanes = lax.broadcasted_iota(jnp.int32, (SKEL, width), 1)
    out_ref[...] = jnp.where(lanes < features, skel, skel + total).astype(BF)


def tree_kernel(points_ref, weights_ref, order_ref, wanted_ref, tree_ref, send_ref, rows_ref, picked_ref):
    turned(points_ref, weights_ref, rows_ref)
    group = 16

    def pick(step, carry):
        base = pl.multiple_of(step * group, group)
        for inner in range(group):
            index = order_ref[base + inner]
            picked_ref[pl.ds(base + inner, 1), :] = rows_ref[pl.ds(index, 1), :]
        return carry

    lax.fori_loop(0, tree_ref.shape[0] // group, pick, 0)
    tree_ref[...] = picked_ref[...].astype(BF)
    leaf = send_ref.shape[1]
    for slot in range(send_ref.shape[0]):
        begin = pl.multiple_of(wanted_ref[slot] * leaf, leaf)
        send_ref[slot] = tree_ref[pl.ds(begin, leaf), :]


def merge_kernel(features, upper_ref, own_ref, other_ref, order_ref, out_ref, rows_ref, rest_ref, skel_ref):
    width = own_ref.shape[1]
    own = own_ref[...].astype(F32)
    other = other_ref[...].astype(F32)
    rows_ref[:SKEL, :] = own
    rows_ref[SKEL:, :] = other
    rest_ref[:SKEL, :] = own
    rest_ref[SKEL:, :] = other
    blank = jnp.zeros((1, width), F32)
    flip = upper_ref[0] * SKEL
    group = 16

    def pick(step, carry):
        for inner in range(group):
            at = step * group + inner
            index = order_ref[at] ^ flip
            skel_ref[pl.ds(at, 1), :] = rows_ref[pl.ds(index, 1), :]
            rest_ref[pl.ds(index, 1), :] = blank
        return carry

    lax.fori_loop(0, SKEL // group, pick, 0)
    skel = skel_ref[...]
    left = left_rows(skel, features)
    total = jnp.zeros((SKEL, width), F32)
    chunk = 512
    for start in range(0, 2 * SKEL, chunk):
        right = right_rows(rows_ref[start : start + chunk, :], features)
        spread = spread_of(lax.dot_general(left, right, NT, preferred_element_type=F32), features)
        total = total + jnp.dot(
            spread, rest_ref[start : start + chunk, :].astype(BF), preferred_element_type=F32
        )
    lanes = lax.broadcasted_iota(jnp.int32, (SKEL, width), 1)
    out_ref[...] = jnp.where(lanes < features, skel, skel + total).astype(BF)


TILE = 256


def add_terms(features, left_ref, sum_ref, begin, leaf, right, value):
    def step(index, carry):
        at = pl.multiple_of(begin + index * TILE, TILE)
        exponent = lax.dot_general(
            left_ref[pl.ds(at, TILE), :], right, NT, preferred_element_type=F32
        )
        dense = dense_of(exponent, features).astype(BF)
        sum_ref[pl.ds(at, TILE), :] += jnp.dot(dense, value, preferred_element_type=F32)
        return carry

    lax.fori_loop(0, leaf // TILE, step, 0, unroll=True)


def far_terms(features, level, far_ref, node_ref, left_ref, sum_ref, leaf):
    value = node_ref[...]
    right = right_rows(value.astype(F32), features)
    for one in range(far_ref.shape[0]):
        @pl.when(far_ref[one, level] > 0)
        def _(one=one):
            add_terms(features, left_ref, sum_ref, one * leaf, leaf, right, value)


def start_kernel(features, far_ref, tree_ref, node_ref, left_ref, sum_ref):
    leaf = tree_ref.shape[0] // far_ref.shape[0]
    for start in range(0, tree_ref.shape[0], 512):
        left_ref[start : start + 512, :] = left_rows(
            tree_ref[start : start + 512, :].astype(F32), features
        )
    sum_ref[...] = jnp.zeros_like(sum_ref)
    far_terms(features, 0, far_ref, node_ref, left_ref, sum_ref, leaf)


def near_kernel(features, target_ref, near_ref, left_ref, prior_ref, sum_ref):
    leaf = near_ref.shape[1]
    sum_ref[...] = prior_ref[...]

    def one_slot(slot, carry):
        target = target_ref[slot]

        @pl.when(target >= 0)
        def _():
            begin = pl.multiple_of(target * leaf, leaf)
            for start in range(0, leaf, SKEL):
                value = near_ref[slot, start : start + SKEL, :]
                right = right_rows(value.astype(F32), features)
                add_terms(features, left_ref, sum_ref, begin, leaf, right, value)

        return carry

    lax.fori_loop(0, target_ref.shape[0], one_slot, 0)


def far_kernel(features, level, far_ref, node_ref, left_ref, prior_ref, sum_ref):
    leaf = left_ref.shape[0] // far_ref.shape[0]
    sum_ref[...] = prior_ref[...]
    far_terms(features, level, far_ref, node_ref, left_ref, sum_ref, leaf)


def last_kernel(features, level, far_ref, node_ref, left_ref, prior_ref, out_ref, sum_ref):
    leaf = left_ref.shape[0] // far_ref.shape[0]
    sum_ref[...] = prior_ref[...]
    far_terms(features, level, far_ref, node_ref, left_ref, sum_ref, leaf)
    for start in range(0, sum_ref.shape[0], 512):
        out_ref[:, start : start + 512] = sum_ref[start : start + 512, :].T[features:, :]


def cost(elements):
    return pl.CostEstimate(flops=elements * 512, transcendentals=elements, bytes_accessed=4 << 20)


PARAMS = pltpu.CompilerParams(vmem_limit_bytes=48 << 20)


def body(points, weights, point_order, node_order, merge_order, far_list, task_target, task_source):
    count, features = points.shape
    columns = weights.shape[1]
    width = features + columns
    levels = far_list.shape[3]
    leaves = far_list.shape[2]
    leaf = count // leaves
    slabs = task_source.shape[2]
    cap = task_source.shape[3]
    slots = slabs * cap
    points_t, weights_t = points.T, weights.T
    order = point_order[0, 0]
    far = far_list[0, 0]
    target = task_target[0, 0].reshape(slots)
    wanted = lax.all_to_all(task_source[0, 0], "task", split_axis=0, concat_axis=0, tiled=True)

    node = pl.pallas_call(
        functools.partial(level_zero_kernel, features),
        out_shape=jax.ShapeDtypeStruct((SKEL, width), BF),
        in_specs=[VMEM, VMEM, SMEM, SMEM],
        out_specs=VMEM,
        scratch_shapes=[
            pltpu.VMEM((count, width), F32),
            pltpu.VMEM((count, width), F32),
            pltpu.VMEM((SKEL, width), F32),
        ],
        cost_estimate=cost(SKEL * count),
        compiler_params=PARAMS,
        name="level_zero",
    )(points_t, weights_t, order, node_order[0, 0])

    tree, send = pl.pallas_call(
        tree_kernel,
        out_shape=(
            jax.ShapeDtypeStruct((count, width), BF),
            jax.ShapeDtypeStruct((slots, leaf, width), BF),
        ),
        in_specs=[VMEM, VMEM, SMEM, SMEM],
        out_specs=(VMEM, VMEM),
        scratch_shapes=[pltpu.VMEM((count, width), F32), pltpu.VMEM((count, width), F32)],
        cost_estimate=cost(SKEL * count),
        compiler_params=PARAMS,
        name="tree",
    )(points_t, weights_t, order, wanted.reshape(slots))
    arrived = lax.all_to_all(send, "task", split_axis=0, concat_axis=0, tiled=True)

    position = lax.axis_index("leaf")

    def merge(level, own, other):
        upper = (position >> level & 1).reshape(1)
        return pl.pallas_call(
            functools.partial(merge_kernel, features),
            out_shape=jax.ShapeDtypeStruct((SKEL, width), BF),
            in_specs=[SMEM, VMEM, VMEM, SMEM],
            out_specs=VMEM,
            scratch_shapes=[
                pltpu.VMEM((2 * SKEL, width), F32),
                pltpu.VMEM((2 * SKEL, width), F32),
                pltpu.VMEM((SKEL, width), F32),
            ],
            cost_estimate=cost(2 * SKEL * SKEL),
            compiler_params=PARAMS,
            name="merge",
        )(upper, own, other, merge_order[0, 0, level])

    siblings = []
    for level in range(levels):
        other = partner(node, "leaf", level)
        siblings.append(other)
        if level < levels - 1:
            node = merge(level, node, other)

    sums = jax.ShapeDtypeStruct((count, width), F32)
    left, total = pl.pallas_call(
        functools.partial(start_kernel, features),
        out_shape=(jax.ShapeDtypeStruct((count, width), BF), sums),
        in_specs=[SMEM, VMEM, VMEM],
        out_specs=(VMEM, VMEM),
        cost_estimate=cost(SKEL * count),
        compiler_params=PARAMS,
        name="far_first",
    )(far, tree, siblings[0])

    for level in range(1, levels - 1):
        total = pl.pallas_call(
            functools.partial(far_kernel, features, level),
            out_shape=sums,
            in_specs=[SMEM, VMEM, VMEM, VMEM],
            out_specs=VMEM,
            cost_estimate=cost(SKEL * count),
            compiler_params=PARAMS,
            name="far_middle",
        )(far, siblings[level], left, total)

    total = pl.pallas_call(
        functools.partial(near_kernel, features),
        out_shape=sums,
        in_specs=[SMEM, VMEM, VMEM, VMEM],
        out_specs=VMEM,
        cost_estimate=cost(slots * leaf * leaf),
        compiler_params=PARAMS,
        name="near",
    )(target, arrived, left, total)

    out = pl.pallas_call(
        functools.partial(last_kernel, features, levels - 1),
        out_shape=jax.ShapeDtypeStruct((columns, count), F32),
        in_specs=[SMEM, VMEM, VMEM, VMEM],
        out_specs=VMEM,
        scratch_shapes=[pltpu.VMEM((count, width), F32)],
        cost_estimate=cost(SKEL * count),
        compiler_params=PARAMS,
        name="far_last",
    )(far, siblings[levels - 1], left, total)
    return out.T


def solution(mesh):
    return jax.shard_map(
        body,
        mesh=mesh,
        in_specs=(
            P(("leaf", "task"), None),
            P(("leaf", "task"), None),
            P("leaf", "task", None),
            P("leaf", "task", None),
            P("leaf", "task", None, None),
            P("leaf", "task", None, None),
            P("leaf", "task", None, None),
            P("leaf", "task", None, None),
        ),
        out_specs=P(("leaf", "task"), None),
        check_vma=False,
    )
```

time: 123 us -> 75.6 us (0.61); the launches traced: 122 us -> 76.3 us
  local copies, waits for them, and re-layouts: 56.6 us -> 7.21 us
  Pallas kernels: 0 us -> 46.2 us
  matrix products: 34.5 us -> 0 us
  other arithmetic: 16.5 us -> 0.16 us
  blocking collectives: 0 us -> 7.83 us
  waiting for transfers between devices: 0.01 us -> 4.36 us
  starting transfers between devices: 14.3 us -> 10.4 us
    pallas_call x0 -> x8, Pallas kernels: none -> 46.2 us  [the longest x1 11 us: body(): pl.pallas_call(functools.partial(near_kernel, features), out_shape=sums,...]
    gather x6 -> x0, local copies, waits for them, and re-layouts: 36 us -> none  [the longest x1 12.1 us: body(): node = merge_joined(tree[node_order[0, 0]], features)]
    dot_general x14 -> x0, matrix products: 34.5 us -> none  [the longest x3 13.3 us: body(): jnp.dot(dense, other[:, features:], preferred_element_type=jnp.float32)]
    reshape x3 -> x0, local copies, waits for them, and re-layouts: 8.75 us -> none  [body(): far_part.reshape(LEAF_DEV, LEAF_PTS, columns) * flags[:, None, None]]
    all_to_all x0 -> x1, blocking collectives: none -> 7.83 us  [body(): lax.all_to_all(task_source[0, 0], 'task', split_axis=0, concat_axis=0, ti...]
    reduce_sum x18 -> x0, other arithmetic: 7.4 us -> none  [the longest x10 5.85 us: kernel(): right_norm = jnp.sum(jnp.square(right_pts.astype(jnp.float32)), axis=-1)]
    ppermute x3, waiting for transfers between devices: 0.01 us -> 4.36 us  [partner(): return lax.ppermute(value, axis, pairs)]
    all_to_all x2 -> x1, starting transfers between devices: 6.94 us -> 3.52 us  [body(): lax.all_to_all(send, 'task', split_axis=0, concat_axis=0, tiled=True)]
  transfers between devices with their start and end apart: 5 -> 4, of which waited for: 0 -> 1; matrix products, arithmetic and copies ran while one was open for 44% -> 0% of each run, Pallas kernels for 0% -> 44%
where the time goes in v1:
time: 75.6 us; the launch traced here: 76.3 us
  Pallas kernels  46.2 us (61%)
  starting transfers between devices  10.4 us (14%)
  blocking collectives  7.83 us (10%)
  local copies, waits for them, and re-layouts  7.21 us (10%)
  waiting for transfers between devices  4.36 us (6%)
    pallas_call x1, Pallas kernels, body(): pl.pallas_call(functools.partial(near_kernel, features), out_shape=sums,...  11 us
    all_to_all x1, blocking collectives, body(): lax.all_to_all(task_source[0, 0], 'task', split_axis=0, concat_axis=0, ti...  7.83 us
    ppermute x3, starting transfers between devices, partner(): return lax.ppermute(value, axis, pairs)  6.88 us
    pallas_call x1, Pallas kernels, body(): pl.pallas_call(tree_kernel, out_shape=(jax.ShapeDtypeStruct((count, width...  6.73 us
    unnamed x27, local copies, waits for them, and re-layouts  6.46 us
    pallas_call x1, Pallas kernels, body(): pl.pallas_call(functools.partial(level_zero_kernel, features), out_shape=...  6.09 us
    pallas_call x2, Pallas kernels, merge(): pl.pallas_call(functools.partial(merge_kernel, features), out_shape=jax.S...  6.01 us
    pallas_call x1, Pallas kernels, body(): pl.pallas_call(functools.partial(start_kernel, features), out_shape=(jax....  5.65 us
  transfers between devices with their start and end apart: 4, of which 1 were waited for; matrix products, arithmetic and copies ran while one was open for 0% of the time, Pallas kernels for 44%

profile of v1, /device:TPU:0, one launch (start us, length us, event | category | flops | bytes accessed | tf_op | source)
XLA Modules:
  0.0 76.3 jit_solution(2531678027664934693)
XLA Ops:
  0.0 0.7 copy.13
  0.7 7.8 %all_to_all.14 = s32[4,1,1]{2,1,0:T(1,128)S(1)} all-to-all(s32[4,1,1]{2,1,0:T(1,128)S(1)} %copy.13), channel_id=1, replica_groups=mesh['leaf'=8,'task'=4] {'task'}, dimensions={0} | all-to-all | bytes 32 | tf_op jit(solution)/shard_map/all_to_all | solution.py:273
  8.6 0.2 reduce.wanted_ref
  8.7 0.0 copy-start.1
  8.7 1.0 %copy-done.1 = bf16[4096,64]{0,1:T(8,128)(2,1)S(1)} copy-done((bf16[4096,64]{0,1:T(8,128)(2,1)S(1)}, bf16[4096,64]{0,1:T(8,128)(2,1)}, u32[]{:S(2)}) %copy-start.1) | copy-done | bytes 524312
  9.8 0.0 copy-start.3
  9.8 1.0 %copy-done.3 = bf16[4096,64]{0,1:T(8,128)(2,1)S(1)} copy-done((bf16[4096,64]{0,1:T(8,128)(2,1)S(1)}, bf16[4096,64]{0,1:T(8,128)(2,1)}, u32[]{:S(2)}) %copy-start.3) | copy-done | bytes 524312
  10.8 0.0 copy-start.5
  10.8 0.7 copy-done.5
  11.5 0.0 copy-start.2
  11.6 0.0 copy-start.4
  11.6 0.0 copy-start.6
  11.6 0.0 copy-start.7
  11.6 6.7 %tree.1 = (bf16[4096,128]{1,0:T(8,128)(2,1)S(1)}, bf16[4,1024,128]{2,1,0:T(8,128)(2,1)}) custom-call(bf16[64,4096]{1,0:T(8,128)(2,1)S(1)} %bitcast.17, bf16[64,4096]{1,0:T(8,128)(2,1)S(1)} %bitcast.19, s32[4096]{0:T(1024)S(1)} %bitcast.21, s32[4]{0:T(128)S(1)} %reduce.wanted_ref), custom_call_target="tpu_custom_call" | custom-call | flops 1073741824 | bytes 4194304 | tf_op jit(solution)/shard_map/tree/pallas_call | solution.py:290
  18.3 0.0 copy-start.9
  18.3 1.0 %copy-done.9 = bf16[4096,128]{1,0:T(8,128)(2,1)} copy-done((bf16[4096,128]{1,0:T(8,128)(2,1)}, bf16[4096,128]{1,0:T(8,128)(2,1)S(1)}, u32[]{:S(2)}) %copy-start.9) | copy-done | bytes 1048600
  19.3 3.5 %all-to-all-start.1 = ((bf16[4,1024,128]{2,1,0:T(8,128)(2,1)}), bf16[4,1024,128]{2,1,0:T(8,128)(2,1)S(1)}, u32[]{:S(2)}, u32[]{:S(2)}) async-start(bf16[4,1024,128]{2,1,0:T(8,128)(2,1)} %get-tuple-element.11), calls=%async_computation.1 | async-start | bytes 2097152 | tf_op jit(solution)/shard_map/all_to_all | solution.py:303
  22.8 0.0 copy-start.11
  22.8 0.0 copy-done.2
  22.8 0.0 copy-done.4
  22.8 0.0 copy-done.6
  22.8 0.0 copy-done.7
  22.9 0.0 copy-start.12
  22.9 6.1 %level_zero.1.own_ref = bf16[512,128]{1,0:T(8,128)(2,1)S(1)} custom-call(bf16[64,4096]{1,0:T(8,128)(2,1)S(1)} %bitcast.18, bf16[64,4096]{1,0:T(8,128)(2,1)S(1)} %bitcast.20, s32[4096]{0:T(1024)S(1)} %bitcast.22, s32[4096]{0:T(1024)S(1)} %bitcast.23), custom_call_target="tpu_custom_call" | custom-call | flops 1073741824 | bytes 4194304 | tf_op jit(solution)/shard_map/level_zero/pallas_call | solution.py:275
  29.0 1.6 %collective-permute-start = (bf16[512,128]{1,0:T(8,128)(2,1)S(1)}, bf16[512,128]{1,0:T(8,128)(2,1)S(1)}, u32[]{:S(2)}, u32[]{:S(2)}) collective-permute-start(bf16[512,128]{1,0:T(8,128)(2,1)S(1)} %level_zero.1.own_ref), channel_id=1, source_target_pairs={{0,4},{4,0},{8,12},{12,8},{16,20},{20,16},{24,28},{28,24},{1,5},{5... | collective-permute-start | bytes 393224 | tf_op jit(solution)/shard_map/ppermute | solution.py:23
  30.5 0.0 copy-done.11
  30.5 4.4 %collective-permute-done.other_ref.node_ref = bf16[512,128]{1,0:T(8,128)(2,1)S(1)} collective-permute-done((bf16[512,128]{1,0:T(8,128)(2,1)S(1)}, bf16[512,128]{1,0:T(8,128)(2,1)S(1)}, u32[]{:S(2)}, u32[]{:S(2)}) %collective-permute-start) | collective-permute-done | bytes 131104 | tf_op jit(solution)/shard_map/ppermute | solution.py:23
  34.9 3.0 %merge.2.own_ref = bf16[512,128]{1,0:T(8,128)(2,1)S(1)} custom-call(s32[1]{0:T(128)} %bitcast.2.upper_ref, bf16[512,128]{1,0:T(8,128)(2,1)S(1)} %level_zero.1.own_ref, bf16[512,128]{1,0:T(8,128)(2,1)S(1)} %collective-permute-done.other_ref.node_ref, s32[1024]{0:T(1024)S(1)} %bitcast.16), custom_call_target="tpu_custom_call" | custom-call | flops 268435456 | bytes 4194304 | tf_op jit(solution)/shard_map/merge/pallas_call | solution.py:309
  37.9 1.6 %collective-permute-start.1 = (bf16[512,128]{1,0:T(8,128)(2,1)S(1)}, bf16[512,128]{1,0:T(8,128)(2,1)S(1)}, u32[]{:S(2)}, u32[]{:S(2)}) collective-permute-start(bf16[512,128]{1,0:T(8,128)(2,1)S(1)} %merge.2.own_ref), channel_id=1, source_target_pairs={{0,8},{4,12},{8,0},{12,4},{16,24},{20,28},{24,16},{28,20},{1,9},{5... | collective-permute-start | bytes 393224 | tf_op jit(solution)/shard_map/ppermute | solution.py:23
  39.5 0.0 copy-done.12
  39.5 0.1 copy.12
  39.6 0.0 copy-start.10
  39.6 1.2 %copy-done.10 = bf16[4096,128]{1,0:T(8,128)(2,1)S(1)} copy-done((bf16[4096,128]{1,0:T(8,128)(2,1)S(1)}, bf16[4096,128]{1,0:T(8,128)(2,1)}, u32[]{:S(2)}) %copy-start.10) | copy-done | bytes 1048600
  40.8 5.7 %far_first.1 = (bf16[4096,128]{1,0:T(8,128)(2,1)S(1)}, f32[4096,128]{1,0:T(8,128)S(1)}) custom-call(s32[4,3]{1,0:T(4,128)S(1)} %bitcast.12, bf16[4096,128]{1,0:T(8,128)(2,1)S(1)} %copy-done.10, bf16[512,128]{1,0:T(8,128)(2,1)S(1)} %collective-permute-done.other_ref.node_ref), custom_call_target="tpu_custom_call" | custom-call | flops 1073741824 | bytes 4194304 | tf_op jit(solution)/shard_map/far_first/pallas_call | solution.py:332
  46.5 0.0 collective-permute-done.1.other_ref.node_ref
  46.5 3.0 %merge.3 = bf16[512,128]{1,0:T(8,128)(2,1)S(1)} custom-call(s32[1]{0:T(128)} %bitcast.1.upper_ref, bf16[512,128]{1,0:T(8,128)(2,1)S(1)} %merge.2.own_ref, bf16[512,128]{1,0:T(8,128)(2,1)S(1)} %collective-permute-done.1.other_ref.node_ref, s32[1024]{0:T(1024)S(1)} %bitcast.15), custom_call_target="tpu_custom_call" | custom-call | flops 268435456 | bytes 4194304 | tf_op jit(solution)/shard_map/merge/pallas_call | solution.py:309
  49.5 3.7 %collective-permute-start.2 = (bf16[512,128]{1,0:T(8,128)(2,1)S(1)}, bf16[512,128]{1,0:T(8,128)(2,1)S(1)}, u32[]{:S(2)}, u32[]{:S(2)}) collective-permute-start(bf16[512,128]{1,0:T(8,128)(2,1)S(1)} %merge.3), channel_id=1, source_target_pairs={{0,16},{4,20},{8,24},{12,28},{16,0},{20,4},{24,8},{28,12},{1,17},{... | collective-permute-start | bytes 393224 | tf_op jit(solution)/shard_map/ppermute | solution.py:23
  53.2 0.0 copy-start.8
  53.2 5.1 %far_middle.1.prior_ref = f32[4096,128]{1,0:T(8,128)S(1)} custom-call(s32[4,3]{1,0:T(4,128)S(1)} %bitcast.13, bf16[512,128]{1,0:T(8,128)(2,1)S(1)} %collective-permute-done.1.other_ref.node_ref, bf16[4096,128]{1,0:T(8,128)(2,1)S(1)} %get-tuple-element.10.left_ref, f32[4096,128]{1,0:T(8,128)S(1)} %get-tuple-element.12.prior_ref), custom_call_target="tpu_custom_call" | custom-call | flops 1073741824 | bytes 4194304 | tf_op jit(solution)/shard_map/far_middle/pallas_call | solution.py:343
  58.3 0.0 copy-start
  58.3 1.3 %copy-done = f32[4096,128]{1,0:T(8,128)} copy-done((f32[4096,128]{1,0:T(8,128)}, f32[4096,128]{1,0:T(8,128)S(1)}, u32[]{:S(2)}) %copy-start) | copy-done | bytes 2097176
  59.7 0.0 all-to-all-done.1.near_ref
  59.7 0.0 copy-done.8
  59.7 11.0 %near.1.prior_ref = f32[4096,128]{1,0:T(8,128)S(1)} custom-call(s32[4]{0:T(128)S(1)} %bitcast.24, bf16[4,1024,128]{2,1,0:T(8,128)(2,1)S(1)} %all-to-all-done.1.near_ref, bf16[4096,128]{1,0:T(8,128)(2,1)S(1)} %get-tuple-element.10.left_ref, f32[4096,128]{1,0:T(8,128)} %copy-done), custom_call_target="tpu_custom_call" | custom-call | flops 2147483648 | bytes 4194304 | tf_op jit(solution)/shard_map/near/pallas_call | solution.py:353
  70.7 0.0 collective-permute-done.2.node_ref
  70.7 5.7 %far_last.1 = f32[64,4096]{1,0:T(8,128)} custom-call(s32[4,3]{1,0:T(4,128)S(1)} %bitcast.14, bf16[512,128]{1,0:T(8,128)(2,1)S(1)} %collective-permute-done.2.node_ref, bf16[4096,128]{1,0:T(8,128)(2,1)S(1)} %get-tuple-element.10.left_ref, f32[4096,128]{1,0:T(8,128)S(1)} %near.1.prior_ref), custom_call_target="tpu_custom_call" | custom-call | flops 1073741824 | bytes 4194304 | tf_op jit(solution)/shard_map/far_last/pallas_call | solution.py:363
  (1 shorter events, 0.0 us)
Async XLA Ops:
  8.7 1.1 %copy-start.1 = (bf16[4096,64]{0,1:T(8,128)(2,1)S(1)}, bf16[4096,64]{0,1:T(8,128)(2,1)}, u32[]{:S(2)}) copy-start(bf16[4096,64]{0,1:T(8,128)(2,1)} %param.8) | copy-start | bytes 1572868
  9.8 1.0 %copy-start.3 = (bf16[4096,64]{0,1:T(8,128)(2,1)S(1)}, bf16[4096,64]{0,1:T(8,128)(2,1)}, u32[]{:S(2)}) copy-start(bf16[4096,64]{0,1:T(8,128)(2,1)} %param.9) | copy-start | bytes 1572868
  10.8 0.7 copy-start.5
  11.5 11.3 %copy-start.2 = (bf16[4096,64]{0,1:T(8,128)(2,1)S(1)}, bf16[4096,64]{0,1:T(8,128)(2,1)}, u32[]{:S(2)}) copy-start(bf16[4096,64]{0,1:T(8,128)(2,1)} %param.8) | copy-start | bytes 1572868
  11.6 11.3 %copy-start.4 = (bf16[4096,64]{0,1:T(8,128)(2,1)S(1)}, bf16[4096,64]{0,1:T(8,128)(2,1)}, u32[]{:S(2)}) copy-start(bf16[4096,64]{0,1:T(8,128)(2,1)} %param.9) | copy-start | bytes 1572868
  11.6 11.3 %copy-start.6 = (s32[1,1,4096]{2,1,0:T(1,128)S(1)}, s32[1,1,4096]{2,1,0:T(1,128)}, u32[]{:S(2)}) copy-start(s32[1,1,4096]{2,1,0:T(1,128)} %param.10) | copy-start | bytes 49156
  11.6 11.3 %copy-start.7 = (s32[1,1,4096]{2,1,0:T(1,128)S(1)}, s32[1,1,4096]{2,1,0:T(1,128)}, u32[]{:S(2)}) copy-start(s32[1,1,4096]{2,1,0:T(1,128)} %param.11) | copy-start | bytes 49156
  18.3 1.0 %copy-start.9 = (bf16[4096,128]{1,0:T(8,128)(2,1)}, bf16[4096,128]{1,0:T(8,128)(2,1)S(1)}, u32[]{:S(2)}) copy-start(bf16[4096,128]{1,0:T(8,128)(2,1)S(1)} %get-tuple-element.9.tree_ref) | copy-start | bytes 3145732
  19.3 40.4 %all-to-all-start.1 = ((bf16[4,1024,128]{2,1,0:T(8,128)(2,1)}), bf16[4,1024,128]{2,1,0:T(8,128)(2,1)S(1)}, u32[]{:S(2)}, u32[]{:S(2)}) async-start(bf16[4,1024,128]{2,1,0:T(8,128)(2,1)} %get-tuple-element.11), calls=%async_computation.1 | async-start | bytes 2097152 | tf_op jit(solution)/shard_map/all_to_all | solution.py:303
  22.8 7.7 %copy-start.11 = (s32[1,1,2,1024]{3,2,1,0:T(2,128)S(1)}, s32[1,1,2,1024]{3,2,1,0:T(2,128)}, u32[]{:S(2)}) copy-start(s32[1,1,2,1024]{3,2,1,0:T(2,128)} %param.12) | copy-start | bytes 24580
  22.9 16.7 %copy-start.12 = (s32[1,1,4,3]{2,1,3,0:T(1,128)S(1)}, s32[1,1,4,3]{2,1,3,0:T(1,128)}, u32[]{:S(2)}) copy-start(s32[1,1,4,3]{2,1,3,0:T(1,128)} %param.13) | copy-start | bytes 148
  29.0 5.9 %collective-permute-start = (bf16[512,128]{1,0:T(8,128)(2,1)S(1)}, bf16[512,128]{1,0:T(8,128)(2,1)S(1)}, u32[]{:S(2)}, u32[]{:S(2)}) collective-permute-start(bf16[512,128]{1,0:T(8,128)(2,1)S(1)} %level_zero.1.own_ref), channel_id=1, source_target_pairs={{0,4},{4,0},{8,12},{12,8},{16,20},{20,16},{24,28},{28,24},{1,5},{5... | collective-permute-start | bytes 393224 | tf_op jit(solution)/shard_map/ppermute | solution.py:23
  37.9 8.6 %collective-permute-start.1 = (bf16[512,128]{1,0:T(8,128)(2,1)S(1)}, bf16[512,128]{1,0:T(8,128)(2,1)S(1)}, u32[]{:S(2)}, u32[]{:S(2)}) collective-permute-start(bf16[512,128]{1,0:T(8,128)(2,1)S(1)} %merge.2.own_ref), channel_id=1, source_target_pairs={{0,8},{4,12},{8,0},{12,4},{16,24},{20,28},{24,16},{28,20},{1,9},{5... | collective-permute-start | bytes 393224 | tf_op jit(solution)/shard_map/ppermute | solution.py:23
  39.6 1.2 %copy-start.10 = (bf16[4096,128]{1,0:T(8,128)(2,1)S(1)}, bf16[4096,128]{1,0:T(8,128)(2,1)}, u32[]{:S(2)}) copy-start(bf16[4096,128]{1,0:T(8,128)(2,1)} %copy-done.9) | copy-start | bytes 3145732
  49.5 21.2 %collective-permute-start.2 = (bf16[512,128]{1,0:T(8,128)(2,1)S(1)}, bf16[512,128]{1,0:T(8,128)(2,1)S(1)}, u32[]{:S(2)}, u32[]{:S(2)}) collective-permute-start(bf16[512,128]{1,0:T(8,128)(2,1)S(1)} %merge.3), channel_id=1, source_target_pairs={{0,16},{4,20},{8,24},{12,28},{16,0},{20,4},{24,8},{28,12},{1,17},{... | collective-permute-start | bytes 393224 | tf_op jit(solution)/shard_map/ppermute | solution.py:23
  53.2 6.5 %copy-start.8 = (s32[1,1,4,1]{2,3,1,0:T(1,128)S(1)}, s32[1,1,4,1]{2,3,1,0:T(1,128)}, u32[]{:S(2)}) copy-start(s32[1,1,4,1]{2,3,1,0:T(1,128)} %param.14) | copy-start | bytes 52
  58.3 1.3 %copy-start = (f32[4096,128]{1,0:T(8,128)}, f32[4096,128]{1,0:T(8,128)S(1)}, u32[]{:S(2)}) copy-start(f32[4096,128]{1,0:T(8,128)S(1)} %far_middle.1.prior_ref) | copy-start | bytes 6291460

commit v2 on v0

v2 whole, which is shorter than its diff:
```python
import functools
import math

import jax
import jax.numpy as jnp
from jax import lax
from jax.experimental import pallas as pl
from jax.experimental.pallas import tpu as pltpu
from jax.sharding import PartitionSpec as P

SKEL = 512
KERNEL_SCALE = 1.5
BF = jnp.bfloat16
F32 = jnp.float32

VMEM = pl.BlockSpec(memory_space=pltpu.VMEM)
SMEM = pl.BlockSpec(memory_space=pltpu.SMEM)


def pieces(norm):
    first = norm.astype(BF).astype(F32)
    left = norm - first
    second = left.astype(BF).astype(F32)
    third = left - second
    return first, second, third


def row_norms(rows, features):
    width = rows.shape[1]
    square = rows * rows
    high = square.astype(BF)
    low = (square - high.astype(F32)).astype(BF)
    picks = (lax.broadcasted_iota(jnp.int32, (width, width), 0) < features).astype(F32).astype(BF)
    return jnp.dot(high, picks, preferred_element_type=F32) + jnp.dot(
        low, picks, preferred_element_type=F32
    )


def placed(lanes, features, body, parts, ones_first):
    first, second, third = parts
    a, b = (3, 0) if ones_first else (0, 3)
    out = jnp.where(lanes < features, body, 0.0)
    out = jnp.where(lanes == features + a, -first, out)
    out = jnp.where(lanes == features + a + 1, -second, out)
    out = jnp.where(lanes == features + a + 2, -third, out)
    ones = (lanes >= features + b) & (lanes < features + b + 3)
    return jnp.where(ones, 1.0, out).astype(BF)


def left_rows(rows, features):
    lanes = lax.broadcasted_iota(jnp.int32, rows.shape, 1)
    return placed(lanes, features, 2.0 * rows, pieces(row_norms(rows, features)), False)


def right_rows(rows, features):
    lanes = lax.broadcasted_iota(jnp.int32, rows.shape, 1)
    return placed(lanes, features, rows, pieces(row_norms(rows, features)), True)


NT = (((1,), (1,)), ((), ()))


def dense_of(exponent, features):
    return jnp.exp2(exponent * (KERNEL_SCALE / features * math.log2(math.e)))


def spread_of(exponent, features, kept):
    dense = dense_of(exponent, features)
    return (dense * (kept / jnp.sum(dense, axis=0, keepdims=True))).astype(BF)


def kept_columns(index_ref, start, count):
    step = index_ref.shape[1]
    found = []
    for base in range(start, start + count, step):
        lanes = lax.broadcasted_iota(jnp.int32, index_ref.shape, 1) + base
        hit = jnp.where(index_ref[...] == lanes, 0.0, 1.0)
        found.append(jnp.min(hit, axis=0, keepdims=True))
    return jnp.concatenate(found, axis=1)


def turned(points_ref, weights_ref, rows_ref):
    step = SKEL
    for start in range(0, rows_ref.shape[0], step):
        both = jnp.concatenate(
            [points_ref[:, start : start + step], weights_ref[:, start : start + step]], axis=0
        )
        rows_ref[start : start + step, :] = both.astype(F32).T


GROUP = 16


def pick_skeleton(index_of, rows_ref, skel_ref, index_ref):
    width = rows_ref.shape[1]

    def pick(step, carry):
        base = pl.multiple_of(step * GROUP, GROUP)
        for inner in range(GROUP):
            index = index_of(base + inner)
            skel_ref[pl.ds(base + inner, 1), :] = rows_ref[index][None]
            index_ref[pl.ds(base + inner, 1), :] = jnp.full((1, width), index, jnp.int32)
        return carry

    lax.fori_loop(0, SKEL // GROUP, pick, 0)


def with_total(skel, total, features):
    lanes = lax.broadcasted_iota(jnp.int32, skel.shape, 1)
    return jnp.where(lanes < features, skel, skel + total).astype(BF)


def level_zero(features, points_ref, rows_ref, skel_ref, index_ref):
    count = points_ref.shape[1]
    skel = skel_ref[...]
    left = left_rows(skel, features)
    width = rows_ref.shape[1]
    chunk = SKEL
    total = jnp.zeros((SKEL, width), F32)
    for start in range(0, count, chunk):
        part = points_ref[:, start : start + chunk].astype(F32)
        norm = jnp.sum(part * part, axis=0, keepdims=True)
        first, second, third = pieces(norm)
        lines = lax.broadcasted_iota(jnp.int32, (width - features, chunk), 0)
        tail = jnp.where(lines < 3, 1.0, 0.0)
        tail = jnp.where(lines == 3, -first, tail)
        tail = jnp.where(lines == 4, -second, tail)
        tail = jnp.where(lines == 5, -third, tail)
        right = jnp.concatenate([part, tail], axis=0).astype(BF)
        kept = kept_columns(index_ref, start, chunk)
        spread = spread_of(jnp.dot(left, right, preferred_element_type=F32), features, kept)
        total = total + jnp.dot(
            spread, rows_ref[start : start + chunk, :].astype(BF), preferred_element_type=F32
        )
    return with_total(skel, total, features)


def merged(features, rows_ref, skel_ref, index_ref):
    skel = skel_ref[...]
    left = left_rows(skel, features)
    total = jnp.zeros(skel.shape, F32)
    for start in range(0, 2 * SKEL, SKEL):
        rows = rows_ref[start : start + SKEL, :]
        right = right_rows(rows, features)
        exponent = lax.dot_general(left, right, NT, preferred_element_type=F32)
        spread = spread_of(exponent, features, kept_columns(index_ref, start, SKEL))
        total = total + jnp.dot(spread, rows.astype(BF), preferred_element_type=F32)
    return with_total(skel, total, features)


TILE = 256


def add_terms(features, left_ref, sum_ref, begin, leaf, right, value):
    def step(index, carry):
        at = pl.multiple_of(begin + index * TILE, TILE)
        exponent = lax.dot_general(
            left_ref[pl.ds(at, TILE), :], right, NT, preferred_element_type=F32
        )
        dense = dense_of(exponent, features).astype(BF)
        sum_ref[pl.ds(at, TILE), :] += jnp.dot(dense, value, preferred_element_type=F32)
        return carry

    lax.fori_loop(0, leaf // TILE, step, 0, unroll=True)


MESH = pl.DeviceIdType.MESH


def chain_kernel(features, levels, slabs, points_ref, weights_ref, order_ref, node_order_ref, merge_ref,
                 far_ref, source_ref, left_ref, sum_ref, near_ref, last_ref,
                 rows_ref, picked_ref, pair_ref, skel_ref, index_ref, node_ref, held_ref,
                 asked_ref, send_ref, node_send, node_recv, ask_send, ask_recv, near_send, near_recv):
    region = lax.axis_index("leaf")
    slab = lax.axis_index("task")
    count = rows_ref.shape[0]
    leaves = far_ref.shape[0]
    leaf = count // leaves
    cap = source_ref.shape[1]

    def bit(level):
        return region // 2**level % 2

    def sibling(level):
        return region + (1 - 2 * bit(level)) * 2**level

    def ahead(step):
        return lax.rem(slab + step, slabs)

    def behind(step):
        return lax.rem(slab + slabs - step, slabs)

    barrier = pltpu.get_barrier_semaphore()
    for level in range(levels):
        pl.semaphore_signal(barrier, inc=1, device_id=(sibling(level), slab), device_id_type=MESH)
    for step in range(1, slabs):
        pl.semaphore_signal(barrier, inc=1, device_id=(region, ahead(step)), device_id_type=MESH)

    turned(points_ref, weights_ref, rows_ref)
    pick_skeleton(lambda at: order_ref[node_order_ref[at]], rows_ref, skel_ref, index_ref)
    node_ref[0] = level_zero(features, points_ref, rows_ref, skel_ref, index_ref)

    pl.semaphore_wait(barrier, levels + slabs - 1)

    def node_copy(level):
        return pltpu.make_async_remote_copy(
            src_ref=node_ref.at[level],
            dst_ref=held_ref.at[level],
            send_sem=node_send.at[level],
            recv_sem=node_recv.at[level],
            device_id=(sibling(level), slab),
            device_id_type=MESH,
        )

    def ask_copy(step):
        return pltpu.make_async_remote_copy(
            src_ref=source_ref,
            dst_ref=asked_ref.at[step],
            send_sem=ask_send.at[step],
            recv_sem=ask_recv.at[step],
            device_id=(region, ahead(step)),
            device_id_type=MESH,
        )

    def near_copy(step):
        return pltpu.make_async_remote_copy(
            src_ref=send_ref.at[step],
            dst_ref=near_ref.at[step],
            send_sem=near_send.at[step],
            recv_sem=near_recv.at[step],
            device_id=(region, behind(step)),
            device_id_type=MESH,
        )

    node_copy(0).start()
    for step in range(1, slabs):
        ask_copy(step).start()

    def pick(step, carry):
        base = pl.multiple_of(step * GROUP, GROUP)
        for inner in range(GROUP):
            index = order_ref[base + inner]
            picked_ref[pl.ds(base + inner, 1), :] = rows_ref[index][None]
        return carry

    lax.fori_loop(0, count // GROUP, pick, 0)

    def fill(slot_ref, step, table):
        at_row = lax.broadcasted_iota(jnp.int32, table.shape, 0) == slab
        at_column = lax.broadcasted_iota(jnp.int32, table.shape, 1)
        for one in range(cap):
            wanted = jnp.max(
                jnp.where(at_row & (at_column == one), table, 0).astype(F32), axis=(0, 1), keepdims=True
            )
            for start in range(0, leaf, TILE):
                rows = picked_ref[start : start + TILE, :]
                for other in range(1, leaves):
                    begin = other * leaf + start
                    rows = jnp.where(wanted == other, picked_ref[begin : begin + TILE, :], rows)
                slot_ref[step, one * leaf + start : one * leaf + start + TILE, :] = rows.astype(BF)

    for step in range(1, slabs):
        ask_copy(step).wait_recv()
        fill(send_ref, step, asked_ref[step])
        near_copy(step).start()
    fill(near_ref, 0, source_ref[...])

    def far_terms(level):
        value = held_ref[level]
        right = right_rows(value.astype(F32), features)
        for one in range(leaves):
            flag = far_ref[one, level].astype(F32)
            weight = (value.astype(F32) * flag).astype(BF)
            add_terms(features, left_ref, sum_ref, one * leaf, leaf, right, weight)

    for level in range(levels):
        node_copy(level).wait_recv()
        if level == levels - 1:
            break
        upper = bit(level)
        pair_ref[pl.ds(pl.multiple_of(upper * SKEL, SKEL), SKEL), :] = node_ref[level].astype(F32)
        pair_ref[pl.ds(pl.multiple_of((1 - upper) * SKEL, SKEL), SKEL), :] = held_ref[level].astype(F32)
        pick_skeleton(lambda at: merge_ref[level, at], pair_ref, skel_ref, index_ref)
        node_ref[level + 1] = merged(features, pair_ref, skel_ref, index_ref)
        node_copy(level + 1).start()
        if level == 0:
            for start in range(0, count, SKEL):
                left_ref[start : start + SKEL, :] = left_rows(picked_ref[start : start + SKEL, :], features)
            sum_ref[...] = jnp.zeros_like(sum_ref)
        far_terms(level)
    last_ref[...] = held_ref[levels - 1]
    for level in range(levels):
        node_copy(level).wait_send()
    for step in range(1, slabs):
        ask_copy(step).wait_send()
        near_copy(step).wait_send()
        near_copy(step).wait_recv()


def last_kernel(features, level, slabs, slab_ref, far_ref, target_ref, node_ref, left_ref, near_ref,
                prior_ref, out_ref, sum_ref):
    leaves = far_ref.shape[0]
    leaf = left_ref.shape[0] // leaves
    sum_ref[...] = prior_ref[...]
    value = node_ref[...]
    right = right_rows(value.astype(F32), features)
    for one in range(leaves):
        @pl.when(far_ref[one, level] > 0)
        def _(one=one):
            add_terms(features, left_ref, sum_ref, one * leaf, leaf, right, value)

    def one_slab(step, carry):
        owner = lax.rem(slab_ref[0] + step, slabs)
        for one in range(target_ref.shape[1]):
            target = target_ref[owner, one]

            @pl.when(target >= 0)
            def _():
                begin = pl.multiple_of(target * leaf, leaf)
                for start in range(0, leaf, SKEL):
                    value = near_ref[step, one * leaf + start : one * leaf + start + SKEL, :]
                    right = right_rows(value.astype(F32), features)
                    add_terms(features, left_ref, sum_ref, begin, leaf, right, value)

        return carry

    lax.fori_loop(0, slabs, one_slab, 0)
    for start in range(0, sum_ref.shape[0], SKEL):
        out_ref[:, start : start + SKEL] = sum_ref[start : start + SKEL, :].T[features:, :]


def body(points, weights, point_order, node_order, merge_order, far_list, task_target, task_source):
    count, features = points.shape
    columns = weights.shape[1]
    width = features + columns
    levels = far_list.shape[3]
    leaf = count // far_list.shape[2]
    slabs, cap = task_source.shape[2:]
    far = far_list[0, 0]
    source = task_source[0, 0]
    left, total, near, last = pl.pallas_call(
        functools.partial(chain_kernel, features, levels, slabs),
        out_shape=(
            jax.ShapeDtypeStruct((count, width), BF),
            jax.ShapeDtypeStruct((count, width), F32),
            jax.ShapeDtypeStruct((slabs, cap * leaf, width), BF),
            jax.ShapeDtypeStruct((SKEL, width), BF),
        ),
        in_specs=[VMEM, VMEM, SMEM, SMEM, SMEM, SMEM, VMEM],
        out_specs=(VMEM, VMEM, VMEM, VMEM),
        scratch_shapes=[
            pltpu.VMEM((count, width), F32),
            pltpu.VMEM((count, width), F32),
            pltpu.VMEM((2 * SKEL, width), F32),
            pltpu.VMEM((SKEL, width), F32),
            pltpu.VMEM((SKEL, width), jnp.int32),
            pltpu.VMEM((levels, SKEL, width), BF),
            pltpu.VMEM((levels, SKEL, width), BF),
            pltpu.VMEM((slabs, slabs, cap), jnp.int32),
            pltpu.VMEM((slabs, cap * leaf, width), BF),
            pltpu.SemaphoreType.DMA((levels,)),
            pltpu.SemaphoreType.DMA((levels,)),
            pltpu.SemaphoreType.DMA((slabs,)),
            pltpu.SemaphoreType.DMA((slabs,)),
            pltpu.SemaphoreType.DMA((slabs,)),
            pltpu.SemaphoreType.DMA((slabs,)),
        ],
        compiler_params=pltpu.CompilerParams(
            collective_id=0, has_side_effects=True, vmem_limit_bytes=48 << 20
        ),
        name="chain",
    )(points.T, weights.T, point_order[0, 0], node_order[0, 0], merge_order[0, 0], far, source)
    slab = lax.axis_index("task").reshape(1)
    out = pl.pallas_call(
        functools.partial(last_kernel, features, levels - 1, slabs),
        out_shape=jax.ShapeDtypeStruct((columns, count), F32),
        in_specs=[SMEM, SMEM, SMEM, VMEM, VMEM, VMEM, VMEM],
        out_specs=VMEM,
        scratch_shapes=[pltpu.VMEM((count, width), F32)],
        compiler_params=pltpu.CompilerParams(vmem_limit_bytes=48 << 20),
        name="near_and_last",
    )(slab, far, task_target[0, 0], last, left, near, total)
    return out.T


def solution(mesh):
    return jax.shard_map(
        body,
        mesh=mesh,
        in_specs=(
            P(("leaf", "task"), None),
            P(("leaf", "task"), None),
            P("leaf", "task", None),
            P("leaf", "task", None),
            P("leaf", "task", None, None),
            P("leaf", "task", None, None),
            P("leaf", "task", None, None),
            P("leaf", "task", None, None),
        ),
        out_specs=P(("leaf", "task"), None),
        check_vma=False,
    )
```

time: 123 us -> 55.1 us (0.45)
  local copies, waits for them, and re-layouts: 56.6 us -> 6.46 us
  Pallas kernels: 0 us -> 47.8 us
  matrix products: 34.5 us -> 0 us
  other arithmetic: 16.5 us -> 0 us
  starting transfers between devices: 14.3 us -> 0 us
    pallas_call x0 -> x2, Pallas kernels: none -> 47.8 us  [the longest x1 34.1 us: body(): pl.pallas_call(functools.partial(chain_kernel, features, levels, slabs),...]
    gather x6 -> x0, local copies, waits for them, and re-layouts: 36 us -> none  [the longest x1 12.1 us: body(): node = merge_joined(tree[node_order[0, 0]], features)]
    dot_general x14 -> x0, matrix products: 34.5 us -> none  [the longest x3 13.3 us: body(): jnp.dot(dense, other[:, features:], preferred_element_type=jnp.float32)]
    reshape x3 -> x0, local copies, waits for them, and re-layouts: 8.75 us -> none  [body(): far_part.reshape(LEAF_DEV, LEAF_PTS, columns) * flags[:, None, None]]
    reduce_sum x18 -> x0, other arithmetic: 7.4 us -> none  [the longest x10 5.85 us: kernel(): right_norm = jnp.sum(jnp.square(right_pts.astype(jnp.float32)), axis=-1)]
    ppermute x3 -> x0, starting transfers between devices: 7.33 us -> none  [partner(): return lax.ppermute(value, axis, pairs)]
    all_to_all x2 -> x0, starting transfers between devices: 6.94 us -> none  [the longest x1 3.7 us: body(): lax.all_to_all(leaves[requested], 'task', split_axis=0, concat_axis=0, ti...]
    select_n x6 -> x0, other arithmetic: 3.24 us -> none  [the longest x2 1.58 us: body(): jnp.where(upper, jnp.concatenate([other, node], axis=0), jnp.concatenate(...]
  transfers between devices with their start and end apart: 5 -> 0, of which waited for: 0 -> 0; matrix products, arithmetic and copies ran while one was open for 44% -> 0% of each run, Pallas kernels for 0% -> 0%
where the time goes in v2:
time: 55.1 us; the launch traced here: 54.3 us
  Pallas kernels  47.8 us (87%)
  local copies, waits for them, and re-layouts  6.46 us (12%)
    pallas_call x1, Pallas kernels, body(): pl.pallas_call(functools.partial(chain_kernel, features, levels, slabs),...  34.1 us
    pallas_call x1, Pallas kernels, body(): pl.pallas_call(functools.partial(last_kernel, features, levels - 1, slabs...  13.7 us
    unnamed x11, local copies, waits for them, and re-layouts  4.98 us

profile of v2, /device:TPU:0, one launch (start us, length us, event | category | flops | bytes accessed | tf_op | source)
XLA Modules:
  0.0 54.3 jit_solution(11806866553796578217)
XLA Ops:
  0.0 0.8 %copy.9 = s32[1,1,4,3]{3,2,1,0:T(4,128)S(1)} copy(s32[1,1,4,3]{2,1,3,0:T(1,128)} %param.13) | data formatting | bytes 96 | tf_op args[5]
  0.8 0.7 %copy.11.target_ref = s32[4,1]{1,0:T(4,128)S(1)} copy(s32[4,1]{0,1:T(1,128)} %bitcast.17) | data formatting | bytes 32 | tf_op jit(solution)/shard_map/squeeze | solution.py:382
  1.5 0.7 %copy.10.source_ref = s32[4,1]{1,0:T(4,128)S(1)} copy(s32[4,1]{0,1:T(1,128)} %bitcast.18) | data formatting | bytes 32 | tf_op jit(solution)/shard_map/squeeze | solution.py:340
  2.2 0.0 copy-start
  2.3 1.0 %copy-done = bf16[4096,64]{0,1:T(8,128)(2,1)S(1)} copy-done((bf16[4096,64]{0,1:T(8,128)(2,1)S(1)}, bf16[4096,64]{0,1:T(8,128)(2,1)}, u32[]{:S(2)}) %copy-start) | copy-done | bytes 524312
  3.3 0.0 copy-start.1
  3.3 1.0 %copy-done.1 = bf16[4096,64]{0,1:T(8,128)(2,1)S(1)} copy-done((bf16[4096,64]{0,1:T(8,128)(2,1)S(1)}, bf16[4096,64]{0,1:T(8,128)(2,1)}, u32[]{:S(2)}) %copy-start.1) | copy-done | bytes 524312
  4.3 0.0 copy-start.2
  4.3 0.7 %copy-done.2 = s32[1,1,4096]{2,1,0:T(1,128)S(1)} copy-done((s32[1,1,4096]{2,1,0:T(1,128)S(1)}, s32[1,1,4096]{2,1,0:T(1,128)}, u32[]{:S(2)}) %copy-start.2) | copy-done | bytes 16408
  5.1 0.0 copy-start.3
  5.1 0.7 %copy-done.3 = s32[1,1,4096]{2,1,0:T(1,128)S(1)} copy-done((s32[1,1,4096]{2,1,0:T(1,128)S(1)}, s32[1,1,4096]{2,1,0:T(1,128)}, u32[]{:S(2)}) %copy-start.3) | copy-done | bytes 16408
  5.8 0.0 copy-start.4
  5.8 0.7 %copy-done.4 = s32[1,1,2,1024]{3,2,1,0:T(2,128)S(1)} copy-done((s32[1,1,2,1024]{3,2,1,0:T(2,128)S(1)}, s32[1,1,2,1024]{3,2,1,0:T(2,128)}, u32[]{:S(2)}) %copy-start.4) | copy-done | bytes 8216
  6.5 34.1 %chain.1 = (bf16[4096,128]{1,0:T(8,128)(2,1)S(1)}, f32[4096,128]{1,0:T(8,128)S(1)}, bf16[4,1024,128]{2,1,0:T(8,128)(2,1)S(1)}, bf16[512,128]{1,0:T(8,128)(2,1)S(1)}) custom-call(bf16[64,4096]{1,0:T(8,128)(2,1)S(1)} %bitcast.10, bf16[64,4096]{1,0:T(8,128)(2,1)S(1)} %bitcast.11, s32[4096]{0:T(1024)S(1)} %bitcast.14, s32[4096]{0:T(1024)S(1)} %bitcast.15, ...), custom_call_target="tpu_custom_call" | custom-call | tf_op jit(solution)/shard_map/chain/pallas_call | solution.py:341
  40.6 13.7 %near_and_last.1 = f32[64,4096]{1,0:T(8,128)} custom-call(s32[1]{0:T(128)} %bitcast.slab_ref, s32[4,3]{1,0:T(4,128)S(1)} %bitcast.13, s32[4,1]{1,0:T(4,128)S(1)} %copy.11.target_ref, bf16[512,128]{1,0:T(8,128)(2,1)S(1)} %get-tuple-element.9.node_ref, bf16[4096,128]{1,0:T(8,128)(2,1)S(1)} %get-tuple-element.10.left_ref, ...), custom_call_target="tpu_custom_call" | custom-call | tf_op jit(solution)/shard_map/near_and_last/pallas_call | solution.py:374
Async XLA Ops:
  2.2 1.0 %copy-start = (bf16[4096,64]{0,1:T(8,128)(2,1)S(1)}, bf16[4096,64]{0,1:T(8,128)(2,1)}, u32[]{:S(2)}) copy-start(bf16[4096,64]{0,1:T(8,128)(2,1)} %param.8) | copy-start | bytes 1572868
  3.3 1.0 %copy-start.1 = (bf16[4096,64]{0,1:T(8,128)(2,1)S(1)}, bf16[4096,64]{0,1:T(8,128)(2,1)}, u32[]{:S(2)}) copy-start(bf16[4096,64]{0,1:T(8,128)(2,1)} %param.9) | copy-start | bytes 1572868
  4.3 0.7 %copy-start.2 = (s32[1,1,4096]{2,1,0:T(1,128)S(1)}, s32[1,1,4096]{2,1,0:T(1,128)}, u32[]{:S(2)}) copy-start(s32[1,1,4096]{2,1,0:T(1,128)} %param.10) | copy-start | bytes 49156
  5.1 0.7 %copy-start.3 = (s32[1,1,4096]{2,1,0:T(1,128)S(1)}, s32[1,1,4096]{2,1,0:T(1,128)}, u32[]{:S(2)}) copy-start(s32[1,1,4096]{2,1,0:T(1,128)} %param.11) | copy-start | bytes 49156
  5.8 0.7 %copy-start.4 = (s32[1,1,2,1024]{3,2,1,0:T(2,128)S(1)}, s32[1,1,2,1024]{3,2,1,0:T(2,128)}, u32[]{:S(2)}) copy-start(s32[1,1,2,1024]{3,2,1,0:T(2,128)} %param.12) | copy-start | bytes 24580

commit v3 on v2

--- a/solution.py
+++ b/solution.py
@@ -15,6 +15,7 @@
 
 VMEM = pl.BlockSpec(memory_space=pltpu.VMEM)
 SMEM = pl.BlockSpec(memory_space=pltpu.SMEM)
+HBM = pl.BlockSpec(memory_space=pltpu.HBM)
 
 
 def pieces(norm):
@@ -151,32 +152,52 @@
 TILE = 256
 
 
+FAR_TILE = 1024
+
+
 def add_terms(features, left_ref, sum_ref, begin, leaf, right, value):
+    tile = min(FAR_TILE, leaf)
+
     def step(index, carry):
-        at = pl.multiple_of(begin + index * TILE, TILE)
+        at = pl.multiple_of(begin + index * tile, tile)
         exponent = lax.dot_general(
-            left_ref[pl.ds(at, TILE), :], right, NT, preferred_element_type=F32
+            left_ref[pl.ds(at, tile), :], right, NT, preferred_element_type=F32
         )
         dense = dense_of(exponent, features).astype(BF)
-        sum_ref[pl.ds(at, TILE), :] += jnp.dot(dense, value, preferred_element_type=F32)
+        sum_ref[pl.ds(at, tile), :] += jnp.dot(dense, value, preferred_element_type=F32)
         return carry
 
-    lax.fori_loop(0, leaf // TILE, step, 0, unroll=True)
+    lax.fori_loop(0, leaf // tile, step, 0, unroll=True)
 
 
 MESH = pl.DeviceIdType.MESH
 
 
-def chain_kernel(features, levels, slabs, points_ref, weights_ref, order_ref, node_order_ref, merge_ref,
-                 far_ref, source_ref, left_ref, sum_ref, near_ref, last_ref,
+def chain_kernel(features, levels, slabs, points_in, weights_in, order_in, node_order_in, merge_in,
+                 far_in, source_in, left_ref, sum_ref, near_ref, last_ref,
                  rows_ref, picked_ref, pair_ref, skel_ref, index_ref, node_ref, held_ref,
-                 asked_ref, send_ref, node_send, node_recv, ask_send, ask_recv, near_send, near_recv):
+                 asked_ref, send_ref, points_ref, weights_ref, order_ref, node_order_ref,
+                 merge_ref, far_ref, source_ref, input_sem, node_send, node_recv, ask_send, ask_recv, near_send, near_recv):
+    loads = [
+        pltpu.make_async_copy(source, target, input_sem.at[at])
+        for at, (source, target) in enumerate([
+            (points_in, points_ref),
+            (weights_in, weights_ref),
+            (order_in, order_ref),
+            (node_order_in, node_order_ref),
+            (merge_in, merge_ref),
+            (far_in, far_ref),
+            (source_in, source_ref),
+        ])
+    ]
+    for load in loads:
+        load.start()
     region = lax.axis_index("leaf")
     slab = lax.axis_index("task")
     count = rows_ref.shape[0]
-    leaves = far_ref.shape[0]
+    leaves = far_ref.shape[2]
     leaf = count // leaves
-    cap = source_ref.shape[1]
+    cap = source_ref.shape[0]
 
     def bit(level):
         return region // 2**level % 2
@@ -196,6 +217,8 @@
     for step in range(1, slabs):
         pl.semaphore_signal(barrier, inc=1, device_id=(region, ahead(step)), device_id_type=MESH)
 
+    for load in loads:
+        load.wait()
     turned(points_ref, weights_ref, rows_ref)
     pick_skeleton(lambda at: order_ref[node_order_ref[at]], rows_ref, skel_ref, index_ref)
     node_ref[0] = level_zero(features, points_ref, rows_ref, skel_ref, index_ref)
@@ -246,11 +269,11 @@
     lax.fori_loop(0, count // GROUP, pick, 0)
 
     def fill(slot_ref, step, table):
-        at_row = lax.broadcasted_iota(jnp.int32, table.shape, 0) == slab
-        at_column = lax.broadcasted_iota(jnp.int32, table.shape, 1)
+        own = lax.broadcasted_iota(jnp.int32, table.shape, 1) == slab
+        place = lax.broadcasted_iota(jnp.int32, table.shape, 0)
         for one in range(cap):
             wanted = jnp.max(
-                jnp.where(at_row & (at_column == one), table, 0).astype(F32), axis=(0, 1), keepdims=True
+                jnp.where(own & (place == one), table, 0).astype(F32), axis=(0, 1), keepdims=True
             )
             for start in range(0, leaf, TILE):
                 rows = picked_ref[start : start + TILE, :]
@@ -269,7 +292,7 @@
         value = held_ref[level]
         right = right_rows(value.astype(F32), features)
         for one in range(leaves):
-            flag = far_ref[one, level].astype(F32)
+            flag = far_ref[level, 0, one].astype(F32)
             weight = (value.astype(F32) * flag).astype(BF)
             add_terms(features, left_ref, sum_ref, one * leaf, leaf, right, weight)
 
@@ -297,22 +320,30 @@
         near_copy(step).wait_recv()
 
 
-def last_kernel(features, level, slabs, slab_ref, far_ref, target_ref, node_ref, left_ref, near_ref,
-                prior_ref, out_ref, sum_ref):
-    leaves = far_ref.shape[0]
+def last_kernel(features, level, slabs, far_in, target_in, node_ref, left_ref, near_ref,
+                prior_ref, out_ref, sum_ref, far_ref, target_ref, input_sem):
+    loads = [
+        pltpu.make_async_copy(far_in, far_ref, input_sem.at[0]),
+        pltpu.make_async_copy(target_in, target_ref, input_sem.at[1]),
+    ]
+    for load in loads:
+        load.start()
+    leaves = far_ref.shape[2]
     leaf = left_ref.shape[0] // leaves
     sum_ref[...] = prior_ref[...]
     value = node_ref[...]
     right = right_rows(value.astype(F32), features)
+    for load in loads:
+        load.wait()
     for one in range(leaves):
-        @pl.when(far_ref[one, level] > 0)
+        @pl.when(far_ref[level, 0, one] > 0)
         def _(one=one):
             add_terms(features, left_ref, sum_ref, one * leaf, leaf, right, value)
 
     def one_slab(step, carry):
-        owner = lax.rem(slab_ref[0] + step, slabs)
-        for one in range(target_ref.shape[1]):
-            target = target_ref[owner, one]
+        owner = lax.rem(lax.axis_index("task") + step, slabs)
+        for one in range(target_ref.shape[0]):
+            target = target_ref[one, owner]
 
             @pl.when(target >= 0)
             def _():
@@ -329,6 +360,10 @@
         out_ref[:, start : start + SKEL] = sum_ref[start : start + SKEL, :].T[features:, :]
 
 
+def in_hbm(value):
+    return pltpu.with_memory_space_constraint(value, pltpu.HBM)
+
+
 def body(points, weights, point_order, node_order, merge_order, far_list, task_target, task_source):
     count, features = points.shape
     columns = weights.shape[1]
@@ -336,8 +371,9 @@
     levels = far_list.shape[3]
     leaf = count // far_list.shape[2]
     slabs, cap = task_source.shape[2:]
-    far = far_list[0, 0]
-    source = task_source[0, 0]
+    far = far_list.transpose(0, 3, 1, 2)[0]
+    source = task_source[0, 0].T
+    inputs = (points.T, weights.T, point_order[0, 0], node_order[0, 0], merge_order[0, 0], far, source)
     left, total, near, last = pl.pallas_call(
         functools.partial(chain_kernel, features, levels, slabs),
         out_shape=(
@@ -346,7 +382,7 @@
             jax.ShapeDtypeStruct((slabs, cap * leaf, width), BF),
             jax.ShapeDtypeStruct((SKEL, width), BF),
         ),
-        in_specs=[VMEM, VMEM, SMEM, SMEM, SMEM, SMEM, VMEM],
+        in_specs=[HBM] * 7,
         out_specs=(VMEM, VMEM, VMEM, VMEM),
         scratch_shapes=[
             pltpu.VMEM((count, width), F32),
@@ -356,8 +392,16 @@
             pltpu.VMEM((SKEL, width), jnp.int32),
             pltpu.VMEM((levels, SKEL, width), BF),
             pltpu.VMEM((levels, SKEL, width), BF),
-            pltpu.VMEM((slabs, slabs, cap), jnp.int32),
+            pltpu.VMEM((slabs, cap, slabs), jnp.int32),
             pltpu.VMEM((slabs, cap * leaf, width), BF),
+            pltpu.VMEM((features, count), BF),
+            pltpu.VMEM((columns, count), BF),
+            pltpu.SMEM((count,), jnp.int32),
+            pltpu.SMEM((count,), jnp.int32),
+            pltpu.SMEM((levels - 1, 2 * SKEL), jnp.int32),
+            pltpu.SMEM(far.shape, jnp.int32),
+            pltpu.VMEM(source.shape, jnp.int32),
+            pltpu.SemaphoreType.DMA((7,)),
             pltpu.SemaphoreType.DMA((levels,)),
             pltpu.SemaphoreType.DMA((levels,)),
             pltpu.SemaphoreType.DMA((slabs,)),
@@ -369,17 +413,22 @@
             collective_id=0, has_side_effects=True, vmem_limit_bytes=48 << 20
         ),
         name="chain",
-    )(points.T, weights.T, point_order[0, 0], node_order[0, 0], merge_order[0, 0], far, source)
-    slab = lax.axis_index("task").reshape(1)
+    )(*[in_hbm(one) for one in inputs])
+    target = task_target[0, 0].T
     out = pl.pallas_call(
         functools.partial(last_kernel, features, levels - 1, slabs),
         out_shape=jax.ShapeDtypeStruct((columns, count), F32),
-        in_specs=[SMEM, SMEM, SMEM, VMEM, VMEM, VMEM, VMEM],
+        in_specs=[HBM, HBM, VMEM, VMEM, VMEM, VMEM],
         out_specs=VMEM,
-        scratch_shapes=[pltpu.VMEM((count, width), F32)],
+        scratch_shapes=[
+            pltpu.VMEM((count, width), F32),
+            pltpu.SMEM(far.shape, jnp.int32),
+            pltpu.SMEM(target.shape, jnp.int32),
+            pltpu.SemaphoreType.DMA((2,)),
+        ],
         compiler_params=pltpu.CompilerParams(vmem_limit_bytes=48 << 20),
         name="near_and_last",
-    )(slab, far, task_target[0, 0], last, left, near, total)
+    )(in_hbm(far), in_hbm(target), last, left, near, total)
     return out.T
 
 

time: 55.1 us -> 44.7 us (0.81)
  the two profiles are of different devices: /device:TPU:0 before, /device:TPU:4 now
where the time goes in v3:
time: 44.7 us; the launch traced here: 44.3 us
  Pallas kernels  44.2 us (99%)
    pallas_call x1, Pallas kernels, body(): pl.pallas_call(functools.partial(chain_kernel, features, levels, slabs),...  32.4 us
    pallas_call x1, Pallas kernels, body(): pl.pallas_call(functools.partial(last_kernel, features, levels - 1, slabs...  11.8 us

profile of v3, /device:TPU:4, one launch (start us, length us, event | category | flops | bytes accessed | tf_op | source)
XLA Modules:
  0.0 44.3 jit_solution(11273747249864457317)
XLA Ops:
  0.0 32.4 %chain.1 = (bf16[4096,128]{1,0:T(8,128)(2,1)S(1)}, f32[4096,128]{1,0:T(8,128)S(1)}, bf16[4,1024,128]{2,1,0:T(8,128)(2,1)S(1)}, bf16[512,128]{1,0:T(8,128)(2,1)S(1)}) custom-call(bf16[64,4096]{1,0:T(8,128)(2,1)} %bitcast.11, bf16[64,4096]{1,0:T(8,128)(2,1)} %bitcast.12, s32[4096]{0:T(1024)} %bitcast.13, s32[4096]{0:T(1024)} %bitcast.14, s32[2,1024]{1,0:T(2,128)} %bitcast.15, ...), custom_call_target="tpu_custom_call" | custom-call | tf_op jit(solution)/shard_map/chain/pallas_call | solution.py:377
  32.4 11.8 %near_and_last.1 = f32[64,4096]{1,0:T(8,128)} custom-call(s32[3,1,4]{2,1,0:T(1,128)} %bitcast.17, s32[1,4]{1,0:T(1,128)} %bitcast.19, bf16[512,128]{1,0:T(8,128)(2,1)S(1)} %get-tuple-element.9.node_ref, bf16[4096,128]{1,0:T(8,128)(2,1)S(1)} %get-tuple-element.10.left_ref, bf16[4,1024,128]{2,1,0:T(8,128)(2,1)S(1)} %get-tuple-element.11.near_ref, ...), custom_call_target="tpu_custom_call" | custom-call | tf_op jit(solution)/shard_map/near_and_last/pallas_call | solution.py:418
